TPU v7x, 32 devices: a whole 2x2x4 slice. The times are simulated.
32 devices in a mesh: dp: 16 (over z, x, core), mp: 2 (over y).
Axes of the slice: x: 2, y: 2, z: 4, core: 2. Of those that a mesh axis runs over, the one named last changes fastest.
Arguments:
- tokens: bfloat16 [80, 1024, 1024], P('dp'), may hold values from -6 to 6
- cotangent: bfloat16 [80, 1024, 1024], P('dp'), may hold values from -6 to 6
- lengths: int32 [80], P('dp'), may hold values from 64 to 1024, as said below
- first_norm_gain: float32 [1024], replicated, may hold values from 0.5 to 1.5
- first_norm_bias: float32 [1024], replicated, may hold values from -2 to 2
- query_key_value_weight: bfloat16 [3, 1024, 1024], P(None, None, 'mp'), may hold values from -0.1875 to 0.1875
- attention_output_weight: bfloat16 [1024, 1024], P('mp'), may hold values from -3 to 3
- attention_output_bias: float32 [1024], replicated, may hold values from -2 to 2
- second_norm_gain: float32 [1024], replicated, may hold values from 0.5 to 1.5
- second_norm_bias: float32 [1024], replicated, may hold values from -2 to 2
- feedforward_up_weight: bfloat16 [1024, 4096], P(None, 'mp'), may hold values from -0.1875 to 0.1875
- feedforward_up_bias: float32 [4096], P('mp'), may hold values from -3 to 3
- feedforward_down_weight: bfloat16 [4096, 1024], P('mp'), may hold values from -0.09375 to 0.09375
- feedforward_down_bias: float32 [1024], replicated, may hold values from -2 to 2
- adapter_down_factor: float32 [2, 1024, 4], replicated, may hold values from -0.1875 to 0.1875
- adapter_up_factor: float32 [2, 4, 1024], replicated, may hold values from -0.3 to 0.3
- down_first_moment: float32 [2, 1024, 4], replicated, may hold values from -0.006 to 0.006
- up_first_moment: float32 [2, 4, 1024], replicated, may hold values from -0.006 to 0.006
- down_second_moment: float32 [2, 1024, 4], replicated, may hold values from 1e-07 to 1e-05
- up_second_moment: float32 [2, 4, 1024], replicated, may hold values from 1e-07 to 1e-05
Outputs:
- block_out: bfloat16 [80, 1024, 1024], P('dp')
- input_grad: bfloat16 [80, 1024, 1024], P('dp')
- new_lora_down: float32 [2, 1024, 4], replicated
- new_lora_up: float32 [2, 4, 1024], replicated
- new_first_down: float32 [2, 1024, 4], replicated
- new_first_up: float32 [2, 4, 1024], replicated
- new_second_down: float32 [2, 1024, 4], replicated
- new_second_up: float32 [2, 4, 1024], replicated
Inputs may be any that keep to these rules, and one draw needn't show every extreme that they name: `lengths`: the first of every 5 sequences (each index of dp's first) has 1024 live tokens.
All inputs are finite; a program needn't handle non-finite values.
Results may differ from a plain program's by a relative error of at most 0.015.
The roundings to bfloat16 on the way count: a program that leaves them out, or rounds other values in their place, can miss the bound.
Values may be sent and summed in bfloat16 or wider, within the bound.
A program may use at most 320 MiB of HBM per device.

v0:
```python
import jax
import jax.numpy as jnp
from jax import lax
from jax.sharding import PartitionSpec as P

HEAD = 64


def layer_norm(values, norm_gain, norm_shift):
    centre = values - jnp.mean(values, axis=-1, keepdims=True)
    spread = jnp.mean(centre * centre, axis=-1, keepdims=True)
    return centre * lax.rsqrt(spread + 1e-05) * norm_gain + norm_shift


def gelu_tanh(values):
    return (
        0.5
        * values
        * (1.0 + jnp.tanh(0.7978845608028654 * (values + 0.044715 * values * values * values)))
    )


def head_major(matrix, seq_rows, head_count):
    return (
        matrix.reshape(seq_rows, -1, head_count, HEAD)
        .transpose(0, 2, 1, 3)
        .reshape(seq_rows * head_count, -1, HEAD)
    )


def token_major(stacked, seq_rows, head_count):
    return (
        stacked.reshape(seq_rows, head_count, -1, HEAD)
        .transpose(0, 2, 1, 3)
        .reshape(-1, head_count * HEAD)
    )


def masked_scores(query_rows, key_rows, seq_len):
    scores = jnp.einsum(
        "qd,kd->qk", query_rows, key_rows, preferred_element_type=jnp.float32
    ) * HEAD ** (-0.5)
    position = jnp.arange(scores.shape[0])
    allowed = (position[None, :] <= position[:, None]) & (position[None, :] < seq_len)
    return jnp.where(allowed, scores, -1e30)


def attend_forward(pieces):
    query_rows, key_rows, value_token_rows, seq_len = pieces
    scores = masked_scores(query_rows, key_rows, seq_len)
    row_max = jnp.max(scores, axis=-1, keepdims=True)
    weights = jnp.exp(scores - row_max)
    row_sum = jnp.sum(weights, axis=-1, keepdims=True)
    probabilities = (weights / row_sum).astype(jnp.bfloat16)
    head_out = jnp.dot(probabilities, value_token_rows, preferred_element_type=jnp.float32)
    return (head_out, row_max[:, 0] + jnp.log(row_sum[:, 0]))


def attend_backward(pieces):
    query_rows, key_rows, value_token_rows, seq_len, grad_head, log_sums = pieces
    scores = masked_scores(query_rows, key_rows, seq_len)
    probabilities = jnp.exp(scores - log_sums[:, None])
    value_gradient_rows = jnp.einsum(
        "qk,qd->kd",
        probabilities.astype(jnp.bfloat16),
        grad_head,
        preferred_element_type=jnp.float32,
    )
    grad_probs = jnp.einsum(
        "qd,kd->qk", grad_head, value_token_rows, preferred_element_type=jnp.float32
    )
    grad_scores = probabilities * (
        grad_probs - jnp.sum(grad_probs * probabilities, axis=-1, keepdims=True)
    )
    grad_scores = grad_scores.astype(jnp.bfloat16)
    query_gradient_rows = jnp.dot(
        grad_scores, key_rows, preferred_element_type=jnp.float32
    ) * HEAD ** (-0.5)
    grad_keys = jnp.einsum(
        "qk,qd->kd", grad_scores, query_rows, preferred_element_type=jnp.float32
    ) * HEAD ** (-0.5)
    return (query_gradient_rows, grad_keys, value_gradient_rows)


def adam_decay_update(adapter, gradient, first_mom, second_mom):
    first_new = 0.9 * first_mom + 0.1 * gradient
    second_new = 0.999 * second_mom + 0.001 * gradient * gradient
    update = first_new / (1.0 - 0.9**10) / (jnp.sqrt(second_new / (1.0 - 0.999**10)) + 1e-08)
    return (adapter - 0.25 * (update + 0.01 * adapter), first_new, second_new)


def per_device(
    tokens,
    cotangent,
    lengths,
    first_norm_gain,
    first_norm_bias,
    query_key_value_weight,
    attention_output_weight,
    attention_output_bias,
    second_norm_gain,
    second_norm_bias,
    feedforward_up_weight,
    feedforward_up_bias,
    feedforward_down_weight,
    feedforward_down_bias,
    adapter_down_factor,
    adapter_up_factor,
    down_first_moment,
    up_first_moment,
    down_second_moment,
    up_second_moment,
):
    seq_rows, seq_len_all, model_width = tokens.shape
    tok_count = seq_rows * seq_len_all
    groups = lax.axis_size("mp")
    worker_shard = lax.axis_index("mp")
    shard_width = query_key_value_weight.shape[2]
    head_count = shard_width // HEAD
    adapter_rank_size = adapter_down_factor.shape[2]
    tokens_f32 = tokens.reshape(tok_count, model_width).astype(jnp.float32)
    normalized_rows = layer_norm(tokens_f32, first_norm_gain, first_norm_bias).astype(jnp.bfloat16)
    down_reduced = adapter_down_factor.astype(jnp.bfloat16)
    up_reduced = adapter_up_factor.astype(jnp.bfloat16)
    up_columns = lax.dynamic_slice_in_dim(up_reduced, worker_shard * shard_width, shard_width, 2)
    down_pair = jnp.concatenate((down_reduced[0], down_reduced[1]), axis=1)
    adapter_pair = jnp.dot(normalized_rows, down_pair, preferred_element_type=jnp.float32).astype(
        jnp.bfloat16
    )
    adapter_query_delta = adapter_pair[:, :adapter_rank_size]
    adapter_value_delta = adapter_pair[:, adapter_rank_size:]
    query_rows = (
        jnp.dot(normalized_rows, query_key_value_weight[0], preferred_element_type=jnp.float32)
        + 8.0 * jnp.dot(adapter_query_delta, up_columns[0], preferred_element_type=jnp.float32)
    ).astype(jnp.bfloat16)
    key_rows = jnp.dot(
        normalized_rows, query_key_value_weight[1], preferred_element_type=jnp.float32
    ).astype(jnp.bfloat16)
    value_token_rows = (
        jnp.dot(normalized_rows, query_key_value_weight[2], preferred_element_type=jnp.float32)
        + 8.0 * jnp.dot(adapter_value_delta, up_columns[1], preferred_element_type=jnp.float32)
    ).astype(jnp.bfloat16)
    limits = jnp.repeat(lengths, head_count)
    query_heads = head_major(query_rows, seq_rows, head_count)
    key_heads = head_major(key_rows, seq_rows, head_count)
    value_heads = head_major(value_token_rows, seq_rows, head_count)
    head_out, log_sums = lax.map(attend_forward, (query_heads, key_heads, value_heads, limits))
    attended = token_major(head_out, seq_rows, head_count).astype(jnp.bfloat16)
    attn_share = (
        lax.psum_scatter(
            jnp.dot(attended, attention_output_weight, preferred_element_type=jnp.float32),
            "mp",
            scatter_dimension=0,
            tiled=True,
        )
        + attention_output_bias
    )

    def norm_two(values):
        return layer_norm(values, second_norm_gain, second_norm_bias)

    def norm_one(values):
        return layer_norm(values, first_norm_gain, first_norm_bias)

    attn_full = lax.all_gather(attn_share, "mp", axis=0, tiled=True)
    residual = tokens_f32 + attn_full
    normed_two = norm_two(residual).astype(jnp.bfloat16)
    hidden_pre = (
        jnp.dot(normed_two, feedforward_up_weight, preferred_element_type=jnp.float32)
        + feedforward_up_bias
    )
    hidden = gelu_tanh(hidden_pre).astype(jnp.bfloat16)
    mlp_share = (
        lax.psum_scatter(
            jnp.dot(hidden, feedforward_down_weight, preferred_element_type=jnp.float32).astype(
                jnp.bfloat16
            ),
            "mp",
            scatter_dimension=0,
            tiled=True,
        ).astype(jnp.float32)
        + feedforward_down_bias
    )
    mlp_full = lax.all_gather(mlp_share.astype(jnp.bfloat16), "mp", axis=0, tiled=True).astype(
        mlp_share.dtype
    )
    block_out = (residual + mlp_full).astype(jnp.bfloat16)
    live_mask = (jnp.arange(seq_len_all)[None, :] < lengths[:, None]).reshape(tok_count, 1)
    grad_out = jnp.where(
        live_mask, cotangent.reshape(tok_count, model_width), jnp.zeros((), jnp.bfloat16)
    )
    grad_hidden = jnp.einsum(
        "td,fd->tf", grad_out, feedforward_down_weight, preferred_element_type=jnp.float32
    )
    _, gelu_back = jax.vjp(gelu_tanh, hidden_pre)
    grad_pre = gelu_back(grad_hidden)[0].astype(jnp.bfloat16)
    grad_norm2_share = lax.psum_scatter(
        jnp.einsum(
            "tf,df->td", grad_pre, feedforward_up_weight, preferred_element_type=jnp.float32
        ),
        "mp",
        scatter_dimension=0,
        tiled=True,
    )
    grad_norm2 = lax.all_gather(grad_norm2_share, "mp", axis=0, tiled=True)
    _, norm2_back = jax.vjp(norm_two, residual)
    grad_resid = grad_out.astype(jnp.float32) + norm2_back(grad_norm2)[0]
    grad_resid_low = grad_resid.astype(jnp.bfloat16)
    grad_attended = jnp.einsum(
        "td,ed->te", grad_resid_low, attention_output_weight, preferred_element_type=jnp.float32
    ).astype(jnp.bfloat16)
    grad_head = head_major(grad_attended, seq_rows, head_count)
    head_dq, head_dk, head_dv = lax.map(
        attend_backward, (query_heads, key_heads, value_heads, limits, grad_head, log_sums)
    )
    query_gradient_rows = token_major(head_dq, seq_rows, head_count).astype(jnp.bfloat16)
    grad_keys = token_major(head_dk, seq_rows, head_count).astype(jnp.bfloat16)
    value_gradient_rows = token_major(head_dv, seq_rows, head_count).astype(jnp.bfloat16)
    adapter_query_gradient = 8.0 * jnp.einsum(
        "te,re->tr", query_gradient_rows, up_columns[0], preferred_element_type=jnp.float32
    )
    adapter_value_gradient = 8.0 * jnp.einsum(
        "te,re->tr", value_gradient_rows, up_columns[1], preferred_element_type=jnp.float32
    )
    adapter_gradient = jnp.concatenate((adapter_query_gradient, adapter_value_gradient), axis=1)
    down_pair_float32 = down_pair.astype(jnp.float32)
    partial_sum = jnp.einsum(
        "te,de->td",
        query_gradient_rows,
        query_key_value_weight[0],
        preferred_element_type=jnp.float32,
    )
    partial_sum = partial_sum + jnp.einsum(
        "te,de->td", grad_keys, query_key_value_weight[1], preferred_element_type=jnp.float32
    )
    partial_sum = partial_sum + jnp.einsum(
        "te,de->td",
        value_gradient_rows,
        query_key_value_weight[2],
        preferred_element_type=jnp.float32,
    )
    grad_norm1_share = lax.psum_scatter(
        partial_sum
        + jnp.einsum(
            "gy,wy->gw", adapter_gradient, down_pair_float32, precision=lax.Precision.HIGHEST
        ),
        "mp",
        scatter_dimension=0,
        tiled=True,
    )
    grad_down_both = jnp.einsum(
        "fi,fg->ig",
        normalized_rows.astype(jnp.float32),
        adapter_gradient,
        precision=lax.Precision.HIGHEST,
    )
    grad_down = jnp.stack(
        (grad_down_both[:, :adapter_rank_size], grad_down_both[:, adapter_rank_size:])
    )
    grad_up_query = 8.0 * jnp.einsum(
        "zm,zj->mj", adapter_query_delta, query_gradient_rows, preferred_element_type=jnp.float32
    )
    grad_up_value = 8.0 * jnp.einsum(
        "zm,zj->mj", adapter_value_delta, value_gradient_rows, preferred_element_type=jnp.float32
    )
    up_column_gradient = jnp.stack((grad_up_query, grad_up_value))
    grad_up = lax.dynamic_update_slice_in_dim(
        jnp.zeros(adapter_up_factor.shape, jnp.float32),
        up_column_gradient,
        worker_shard * shard_width,
        2,
    )
    live_local = jnp.sum(lengths).astype(jnp.float32)
    down_reduced_sum, up_reduced_sum, live_sum = lax.psum(
        (grad_down, grad_up, live_local), ("dp", "mp")
    )
    active_token_total = live_sum / groups
    grad_norm1 = lax.all_gather(grad_norm1_share, "mp", axis=0, tiled=True)
    _, norm1_back = jax.vjp(norm_one, tokens_f32)
    input_grad = (grad_resid + norm1_back(grad_norm1)[0]).astype(jnp.bfloat16)
    down_factor_next, down_first_moment_next, down_second_moment_next = adam_decay_update(
        adapter_down_factor,
        down_reduced_sum / active_token_total,
        down_first_moment,
        down_second_moment,
    )
    up_factor_next, up_first_moment_next, up_second_moment_next = adam_decay_update(
        adapter_up_factor, up_reduced_sum / active_token_total, up_first_moment, up_second_moment
    )
    return (
        block_out.reshape(seq_rows, seq_len_all, model_width),
        input_grad.reshape(seq_rows, seq_len_all, model_width),
        down_factor_next,
        up_factor_next,
        down_first_moment_next,
        up_first_moment_next,
        down_second_moment_next,
        up_second_moment_next,
    )


def solution(mesh):
    in_specs = (
        P("dp", None, None),
        P("dp", None, None),
        P("dp"),
        P(),
        P(),
        P(None, None, "mp"),
        P("mp", None),
        P(),
        P(),
        P(),
        P(None, "mp"),
        P("mp"),
        P("mp", None),
        P(),
        P(),
        P(),
        P(),
        P(),
        P(),
        P(),
    )
    out_specs = (P("dp", None, None), P("dp", None, None), P(), P(), P(), P(), P(), P())
    return jax.shard_map(
        per_device, mesh=mesh, in_specs=in_specs, out_specs=out_specs, check_vma=False
    )
```

profile of v0, /device:TPU:31, one launch (start us, length us, event | category | flops | bytes accessed | tf_op | source)
XLA Modules:
  0.0 3232.9 jit_solution(272353704106513813)
XLA Ops:
  86.5 12.8 reshape.258
  99.3 14.9 copy.59
  130.0 12.7 reshape.262
  142.7 14.9 copy.61
  165.7 12.7 reshape.260
  178.4 14.9 copy.60
  196.5 357.3 %while.26 = (s32[]{:T(128)}, bf16[40,1024,64]{1,2,0:T(8,128)(2,1)}, f32[40,1024]{1,0:T(8,128)}, s32[40]{0:T(128)S(1)}, bf16[40,1024,64]{2,1,0:T(8,128)(2,1)}, /*...) while((s32[]{:T(128)}, bf16[40,1024,64]{1,2,0:T(8,128)(2,1)}, ...), condition=%wide.region_5.6_spmd, body=%wide.region_2.5_spmd.sunk | while | flops 287309824 | bytes 13678705 | solution.py:147
  576.4 234.2 %reduce-scatter.5.cloned.1.call-done = f32[2560,1024]{1,0:T(8,128)} async-done(((f32[5120,1024]{1,0:T(8,128)}), f32[2560,1024]{1,0:T(8,128)}) %reduce-scatter.5.cloned.1.call-update) | async-done | bytes 10485776 | tf_op jit(solution)/shard_map/reduce_scatter | solution.py:150
  831.5 237.2 %all-gather.5.cloned.1.call-done = f32[5120,1024]{1,0:T(8,128)} async-done(((f32[2560,1024]{1,0:T(8,128)}), f32[5120,1024]{1,0:T(8,128)}) %all-gather.5.cloned.1.call-update) | async-done | bytes 20971536 | tf_op jit(solution)/shard_map/all_gather | solution.py:165
  1087.2 32.9 %fusion.77 = f32[5120,2048]{1,0:T(8,128)} fusion(bf16[1024,2048]{1,0:T(8,128)(2,1)} %param.34, f32[5120,1024]{1,0:T(8,128)} %copy-done.1, f32[1024]{0:T(1024)S(1)} %copy-done.48, f32[1024]{0:T(1024)S(1)} %copy-done.38, f32[5120]{0:T(1024)S(1)} %fusion.113, f32[5120]{0:T(1024)S(1)} %broadcast_multiply_fusion.1), kind=kOutput, calls=%fused_computation.102 | convolution fusion | flops 21501050880 | bytes 67158016 | tf_op jit(solution)/shard_map/dot_general | solution.py:169
  1120.1 58.9 %fusion.164 = bf16[5120,2048]{1,0:T(8,128)(2,1)} fusion(f32[5120,2048]{1,0:T(8,128)} %fusion.77, f32[2048]{0:T(1024)S(1)} %copy-done.47, bf16[5120,1024]{1,0:T(8,128)(2,1)} %bitcast_select_fusion, bf16[2048,1024]{1,0:T(8,128)(2,1)} %param.36), kind=kOutput, calls=%fused_computation.67.clone.clone.1 | convolution fusion | flops 21736980480 | bytes 77602816 | tf_op jit(solution)/shard_map/td,fd->tf/dot_general | solution.py:192
  1179.0 28.1 fusion.70
  1207.2 36.4 %fusion.83 = bf16[5120,1024]{1,0:T(8,128)(2,1)} fusion(bf16[2048,1024]{1,0:T(8,128)(2,1)} %param.36, f32[5120,2048]{1,0:T(8,128)} %fusion.77, f32[2048]{0:T(1024)S(1)} %copy-done.47), kind=kOutput, calls=%fused_computation.112 | convolution fusion | flops 21584936960 | bytes 56631296 | tf_op jit(solution)/shard_map/dot_general | solution.py:175
  1243.6 198.0 %reduce-scatter.9.cloned.1.call-done = f32[2560,1024]{1,0:T(8,128)} async-done(((f32[5120,1024]{1,0:T(8,128)}), f32[2560,1024]{1,0:T(8,128)}) %reduce-scatter.9.cloned.1.call-update) | async-done | bytes 10485776 | tf_op jit(solution)/shard_map/reduce_scatter | solution.py:197
  1441.7 124.6 %reduce-scatter.7.cloned.1.call-done = bf16[2560,1024]{1,0:T(8,128)(2,1)} async-done(((bf16[5120,1024]{1,0:T(8,128)(2,1)}), bf16[2560,1024]{1,0:T(8,128)(2,1)}) %reduce-scatter.7.cloned.1.call-update) | async-done | bytes 5242896 | tf_op jit(solution)/shard_map/reduce_scatter | solution.py:174
  1572.8 242.3 %all-gather.9.cloned.1.call-done = f32[5120,1024]{1,0:T(8,128)} async-done(((f32[2560,1024]{1,0:T(8,128)}), f32[5120,1024]{1,0:T(8,128)}) %all-gather.9.cloned.1.call-update) | async-done | bytes 20971536 | tf_op jit(solution)/shard_map/all_gather | solution.py:205
  1815.1 16.7 multiply_reduce_fusion.1
  1831.8 114.8 %all-gather.7.cloned.1.call-done = bf16[5120,1024]{1,0:T(8,128)(2,1)} async-done(((bf16[2560,1024]{1,0:T(8,128)(2,1)}), bf16[5120,1024]{1,0:T(8,128)(2,1)}) %all-gather.7.cloned.1.call-update) | async-done | bytes 10485776 | tf_op jit(solution)/shard_map/all_gather | solution.py:184
  1946.6 29.2 fusion.130
  1976.4 14.9 fusion.84
  1999.2 12.8 reshape.266
  2012.0 14.9 copy.64
  2036.0 551.7 %while.27 = (s32[]{:T(128)}, bf16[40,1024,64]{1,2,0:T(8,128)(2,1)}, bf16[40,1024,64]{1,2,0:T(8,128)(2,1)}, bf16[40,1024,64]{1,2,0:T(8,128)(2,1)}, s32[40]{0:T(12...) while((s32[]{:T(128)}, bf16[40,1024,64]{1,2,0:T(8,128)(2,1)}, ...), condition=%wide.region_15.16_spmd, body=%wide.region_13.15_spmd.sunk | while | flops 682754048 | bytes 34106496 | solution.py:213
  2600.9 12.2 fusion.89
  2626.3 12.2 fusion.96
  2662.5 29.6 add_add_fusion.2
  2692.1 234.4 %reduce-scatter.11.cloned.1.call-done = f32[2560,1024]{1,0:T(8,128)} async-done(((f32[5120,1024]{1,0:T(8,128)}), f32[2560,1024]{1,0:T(8,128)}) %reduce-scatter.11.cloned.1.call-update) | async-done | bytes 10485776 | tf_op jit(solution)/shard_map/reduce_scatter | solution.py:242
  2945.3 41.1 %all-reduce.2 = (f32[2,1024,4]{1,2,0:T(4,128)S(1)}, f32[]{:T(128)}, f32[2,4,1024]{2,1,0:T(4,128)S(1)}) all-reduce(f32[2,1024,4]{1,2,0:T(4,128)S(1)} %pad_maximum_fusion.3, f32[]{:T(128)S(6)} %convert_element_type.187, f32[2,4,1024]{2,1,0:T(4,128)S(1)} %maximum_dynamic-update-slice_fusion), channel_id=1, replica_groups=mesh['dp'=16,'mp'=2] {'dp','mp'}, use_global_device_ids=true, to_apply=%region_19.20 | all-reduce | flops 16385 | bytes 131080 | tf_op jit(solution)/shard_map/psum | solution.py:274
  2988.5 188.6 %all-gather.11.cloned.1.call-done = f32[5120,1024]{1,0:T(8,128)} async-done(((f32[2560,1024]{1,0:T(8,128)}), f32[5120,1024]{1,0:T(8,128)}) %all-gather.11.cloned.1.call-update) | async-done | bytes 20971536 | tf_op jit(solution)/shard_map/all_gather | solution.py:278
  3177.1 13.2 fusion.68
  3190.3 12.7 fusion.127
  3203.1 22.8 add_convert_fusion
  (825 shorter events, 1168.0 us)
Async XLA Ops:
  7.2 559.0 %copy-start = (bf16[512,1024]{1,0:T(8,128)(2,1)S(1)}, bf16[512,1024]{1,0:T(8,128)(2,1)}, u32[]{:S(2)}) copy-start(bf16[512,1024]{1,0:T(8,128)(2,1)} %param.30) | copy-start | bytes 3145732
  7.2 803.5 %reduce-scatter.5.cloned.1.call-start = ((), (), s32[]{:S(2)}) async-start(), calls=%async_computation.4 | async-start | bytes 31457280 | tf_op jit(solution)/shard_map/reduce_scatter | solution.py:150
  19.7 31.7 copy-start.6
  63.9 50.3 %copy-start.24 = (bf16[2,4,512]{2,1,0:T(4,128)(2,1)}, bf16[2,4,512]{2,1,0:T(4,128)(2,1)S(1)}, u32[]{:S(2)}) copy-start(bf16[2,4,512]{2,1,0:T(4,128)(2,1)S(1)} %dynamic-slice_convert_fusion) | copy-start | bytes 24580
  70.7 43.5 %copy-start.4 = (bf16[5120,8]{0,1:T(8,128)(2,1)}, bf16[5120,8]{0,1:T(8,128)(2,1)S(1)}, u32[]{:S(2)}) copy-start(bf16[5120,8]{0,1:T(8,128)(2,1)S(1)} %convolution_convert_fusion.1) | copy-start | bytes 245764
  576.4 234.3 %copy-start.41 = (f32[1024]{0:T(1024)S(1)}, f32[1024]{0:T(1024)}, u32[]{:S(2)}) copy-start(f32[1024]{0:T(1024)} %param.31) | copy-start | bytes 12292
  576.4 492.3 %all-gather.5.cloned.1.call-start = ((), (), s32[]{:S(2)}) async-start(), calls=%async_computation.5 | async-start | bytes 31457280 | tf_op jit(solution)/shard_map/all_gather | solution.py:165
  821.3 620.3 %reduce-scatter.9.cloned.1.call-start = ((), (), s32[]{:S(2)}) async-start(), calls=%async_computation.8 | async-start | bytes 31457280 | tf_op jit(solution)/shard_map/reduce_scatter | solution.py:197
  1087.2 32.9 %copy-start.20 = (f32[5120]{0:T(1024)}, f32[5120]{0:T(1024)S(1)}, u32[]{:S(2)}) copy-start(f32[5120]{0:T(1024)S(1)} %fusion.113) | copy-start | bytes 61444
  1087.2 32.9 %copy-start.47 = (f32[2048]{0:T(1024)S(1)}, f32[2048]{0:T(1024)}, u32[]{:S(2)}) copy-start(f32[2048]{0:T(1024)} %param.35) | copy-start | bytes 24580
  1207.1 359.2 %reduce-scatter.7.cloned.1.call-start = ((), (), s32[]{:S(2)}) async-start(), calls=%async_computation.6 | async-start | bytes 15728640 | tf_op jit(solution)/shard_map/reduce_scatter | solution.py:174
  1243.5 322.8 %copy-start.40 = (f32[1024]{0:T(1024)S(1)}, f32[1024]{0:T(1024)}, u32[]{:S(2)}) copy-start(f32[1024]{0:T(1024)} %param.37) | copy-start | bytes 12292
  1243.6 571.5 %all-gather.9.cloned.1.call-start = ((), (), s32[]{:S(2)}) async-start(), calls=%async_computation.9 | async-start | bytes 31457280 | tf_op jit(solution)/shard_map/all_gather | solution.py:205
  1441.6 373.5 %copy-start.9 = (f32[5120]{0:T(1024)S(1)}, f32[5120]{0:T(1024)}, u32[]{:S(2)}) copy-start(f32[5120]{0:T(1024)} %copy-done.8) | copy-start | bytes 61444
  1441.6 373.5 %copy-start.39 = (f32[1024]{0:T(1024)S(1)}, f32[1024]{0:T(1024)}, u32[]{:S(2)}) copy-start(f32[1024]{0:T(1024)} %param.32) | copy-start | bytes 12292
  1441.6 505.0 %all-gather.7.cloned.1.call-start = ((), (), s32[]{:S(2)}) async-start(), calls=%async_computation.7 | async-start | bytes 15728640 | tf_op jit(solution)/shard_map/all_gather | solution.py:184
  1572.7 1353.8 %reduce-scatter.11.cloned.1.call-start = ((), (), s32[]{:S(2)}) async-start(), calls=%async_computation.10 | async-start | bytes 31457280 | tf_op jit(solution)/shard_map/reduce_scatter | solution.py:242
  1572.8 259.0 %copy-start.13 = (f32[5120]{0:T(1024)S(1)}, f32[5120]{0:T(1024)}, u32[]{:S(2)}) copy-start(f32[5120]{0:T(1024)} %copy-done.12) | copy-start | bytes 61444
  1572.8 373.8 %copy-start.21 = (f32[5120]{0:T(1024)S(1)}, f32[5120]{0:T(1024)}, u32[]{:S(2)}) copy-start(f32[5120]{0:T(1024)} %copy-done.20) | copy-start | bytes 61444
  2692.1 234.5 %copy-start.43 = (s32[5]{0:T(128)S(1)}, s32[5]{0:T(128)}, u32[]{:S(2)}) copy-start(s32[5]{0:T(128)} %param.26) | copy-start | bytes 64
  2692.1 235.7 %copy-start.5 = (bf16[5120,8]{0,1:T(8,128)(2,1)S(1)}, bf16[5120,8]{0,1:T(8,128)(2,1)}, u32[]{:S(2)}) copy-start(bf16[5120,8]{0,1:T(8,128)(2,1)} %copy-done.4) | copy-start | bytes 245764
  2692.1 484.9 %all-gather.11.cloned.1.call-start = ((), (), s32[]{:S(2)}) async-start(), calls=%async_computation.11 | async-start | bytes 31457280 | tf_op jit(solution)/shard_map/all_gather | solution.py:278
  2927.8 59.2 %copy-start.30 = (f32[2,4,1024]{2,1,0:T(4,128)S(1)}, f32[2,4,1024]{2,1,0:T(4,128)}, u32[]{:S(2)}) copy-start(f32[2,4,1024]{2,1,0:T(4,128)} %param.39) | copy-start | bytes 98308
  2927.8 59.2 %copy-start.33 = (f32[2,4,1024]{2,1,0:T(4,128)S(1)}, f32[2,4,1024]{2,1,0:T(4,128)}, u32[]{:S(2)}) copy-start(f32[2,4,1024]{2,1,0:T(4,128)} %param.41) | copy-start | bytes 98308
  2927.9 59.2 %copy-start.34 = (f32[2,4,1024]{2,1,0:T(4,128)S(1)}, f32[2,4,1024]{2,1,0:T(4,128)}, u32[]{:S(2)}) copy-start(f32[2,4,1024]{2,1,0:T(4,128)} %param.43) | copy-start | bytes 98308
  2927.9 59.9 %copy-start.17 = (f32[2,1024,4]{1,2,0:T(4,128)S(1)}, f32[2,1024,4]{1,2,0:T(4,128)}, u32[]{:S(2)}) copy-start(f32[2,1024,4]{1,2,0:T(4,128)} %param.38) | copy-start | bytes 98308
  2927.9 59.9 %copy-start.35 = (f32[2,1024,4]{1,2,0:T(4,128)S(1)}, f32[2,1024,4]{1,2,0:T(4,128)}, u32[]{:S(2)}) copy-start(f32[2,1024,4]{1,2,0:T(4,128)} %param.40) | copy-start | bytes 98308
  2927.9 59.9 %copy-start.36 = (f32[2,1024,4]{1,2,0:T(4,128)S(1)}, f32[2,1024,4]{1,2,0:T(4,128)}, u32[]{:S(2)}) copy-start(f32[2,1024,4]{1,2,0:T(4,128)} %param.42) | copy-start | bytes 98308
  2927.9 249.1 %copy-start.7 = (f32[5120]{0:T(1024)S(1)}, f32[5120]{0:T(1024)}, u32[]{:S(2)}) copy-start(f32[5120]{0:T(1024)} %copy-done.6) | copy-start | bytes 61444
  2927.9 249.1 %copy-start.19 = (f32[1024]{0:T(1024)S(1)}, f32[1024]{0:T(1024)}, u32[]{:S(2)}) copy-start(f32[1024]{0:T(1024)} %param.27) | copy-start | bytes 12292
  2988.5 201.8 %copy-start.15 = (f32[5120]{0:T(1024)S(1)}, f32[5120]{0:T(1024)}, u32[]{:S(2)}) copy-start(f32[5120]{0:T(1024)} %copy-done.14) | copy-start | bytes 61444
  2988.5 201.8 %copy-start.11 = (f32[5120]{0:T(1024)S(1)}, f32[5120]{0:T(1024)}, u32[]{:S(2)}) copy-start(f32[5120]{0:T(1024)} %copy-done.10) | copy-start | bytes 61444
  (28 other events, 318.4 us)
Sparse Core Ops, SparseCore 0:
  576.5 234.1 reduce-scatter.4
  821.4 247.3 all-gather.4
  1207.2 234.2 reduce-scatter.8
  1444.3 121.9 reduce-scatter.6
  1567.7 247.3 all-gather.8
  1817.1 129.4 all-gather.6
  2692.2 234.2 reduce-scatter.10
  2928.1 248.9 all-gather.10
where the time goes:
time: 3260 us; the launch traced here: 3230 us
  waiting for transfers between devices  1570 us (48%)
  matrix products  911 us (28%)
  local copies, waits for them, and re-layouts  344 us (11%)
  other arithmetic  344 us (11%)
  blocking collectives  41.1 us (1%)
    all_gather x1, waiting for transfers between devices, per_device(): grad_norm2 = lax.all_gather(grad_norm2_share, 'mp', axis=0, tiled=True)  242 us
    all_gather x1, waiting for transfers between devices, per_device(): attn_full = lax.all_gather(attn_share, 'mp', axis=0, tiled=True)  237 us
    reduce_scatter x1, waiting for transfers between devices, per_device(): lax.psum_scatter(partial_sum + jnp.einsum('gy,wy->gw', adapter_gradient,...  234 us
    reduce_scatter x1, waiting for transfers between devices, per_device(): lax.psum_scatter(jnp.dot(attended, attention_output_weight, preferred_ele...  234 us
    reduce_scatter x1, waiting for transfers between devices, per_device(): lax.psum_scatter(jnp.einsum('tf,df->td', grad_pre, feedforward_up_weight,...  198 us
    all_gather x1, waiting for transfers between devices, per_device(): grad_norm1 = lax.all_gather(grad_norm1_share, 'mp', axis=0, tiled=True)  189 us
    dot_general x80, matrix products, masked_scores(): jnp.einsum('qd,kd->qk', query_rows, key_rows, preferred_element_type=jnp....  150 us
    reduce_scatter x1, waiting for transfers between devices, per_device(): lax.psum_scatter(jnp.dot(hidden, feedforward_down_weight, preferred_eleme...  125 us
  transfers between devices with their start and end apart: 8, of which 8 were waited for; matrix products, arithmetic and copies ran while one was open for 3% of the time, Pallas kernels for 0%

commit v1 on v0

--- a/solution.py
+++ b/solution.py
@@ -1,6 +1,8 @@
 import jax
 import jax.numpy as jnp
 from jax import lax
+from jax.experimental import pallas as pl
+from jax.experimental.pallas import tpu as pltpu
 from jax.sharding import PartitionSpec as P
 
 HEAD = 64
@@ -299,6 +301,421 @@
     )
 
 
+TILE = 256
+NT = (((1,), (1,)), ((), ()))
+
+
+def head_lanes(half):
+    lane = lax.broadcasted_iota(jnp.int32, (1, 2 * HEAD), 1)
+    return (lane >= half * HEAD) & (lane < (half + 1) * HEAD)
+
+
+def one_head(block, half):
+    return jnp.where(head_lanes(half), block, jnp.zeros((), block.dtype))
+
+
+def edge_allowed(key_start, query_start, seq_len):
+    key_at = key_start + lax.broadcasted_iota(jnp.int32, (TILE, TILE), 0)
+    query_at = query_start + lax.broadcasted_iota(jnp.int32, (TILE, TILE), 1)
+    return (key_at <= query_at) & (key_at < seq_len)
+
+
+def attention_forward_kernel(lens_ref, q_ref, k_ref, v_ref, out_ref, lse_ref, vt_ref):
+    seq_len = lens_ref[pl.program_id(0)]
+    live_tiles = (seq_len + TILE - 1) // TILE
+    vt_ref[...] = v_ref[0].T
+    tiles = q_ref.shape[1] // TILE
+
+    def row_tile(tile, extent):
+        rows = pl.ds(tile * TILE, TILE)
+        inner = (extent - 1) * TILE
+        query = q_ref[0, rows, :] * HEAD ** (-0.5)
+        allowed = edge_allowed(inner, tile * TILE, seq_len)
+        outs = []
+        for half in range(2):
+            mine = one_head(query, half)
+            edge = lax.dot_general(
+                k_ref[0, pl.ds(inner, TILE), :], mine, NT, preferred_element_type=jnp.float32
+            )
+            edge = jnp.where(allowed, edge, -1e30)
+            top = jnp.max(edge, axis=0, keepdims=True)
+            if inner:
+                past = lax.dot_general(
+                    k_ref[0, pl.ds(0, inner), :], mine, NT, preferred_element_type=jnp.float32
+                )
+                top = jnp.maximum(top, jnp.max(past, axis=0, keepdims=True))
+            head_rows = pl.ds(half * HEAD, HEAD)
+            edge = jnp.exp(edge - top)
+            total = jnp.sum(edge, axis=0, keepdims=True)
+            out = jnp.dot(
+                vt_ref[head_rows, pl.ds(inner, TILE)],
+                edge.astype(jnp.bfloat16),
+                preferred_element_type=jnp.float32,
+            )
+            if inner:
+                past = jnp.exp(past - top)
+                total = total + jnp.sum(past, axis=0, keepdims=True)
+                out = out + jnp.dot(
+                    vt_ref[head_rows, pl.ds(0, inner)],
+                    past.astype(jnp.bfloat16),
+                    preferred_element_type=jnp.float32,
+                )
+            outs.append(out / total)
+            lse_ref[0, 0, pl.ds(half, 1), rows] = top + jnp.log(total)
+        out_ref[0, rows, :] = jnp.concatenate(outs, axis=0).T.astype(out_ref.dtype)
+
+    for tile in range(tiles):
+        for extent in range(1, tile + 2):
+            pl.when(jnp.minimum(live_tiles, tile + 1) == extent)(
+                lambda tile=tile, extent=extent: row_tile(tile, extent)
+            )
+
+
+def attention_forward(lens, query, key, value):
+    seqs, length, width = query.shape
+    pairs = width // (2 * HEAD)
+    spec = pl.BlockSpec((1, length, 2 * HEAD), lambda s, h, lens: (s, 0, h))
+    return pl.pallas_call(
+        attention_forward_kernel,
+        grid_spec=pltpu.PrefetchScalarGridSpec(
+            num_scalar_prefetch=1,
+            grid=(seqs, pairs),
+            in_specs=[spec] * 3,
+            out_specs=[spec, pl.BlockSpec((1, 1, 2, length), lambda s, h, lens: (s, h, 0, 0))],
+            scratch_shapes=[pltpu.VMEM((2 * HEAD, length), jnp.bfloat16)],
+        ),
+        out_shape=[
+            jax.ShapeDtypeStruct(query.shape, jnp.bfloat16),
+            jax.ShapeDtypeStruct((seqs, pairs, 2, length), jnp.float32),
+        ],
+        cost_estimate=pl.CostEstimate(
+            flops=seqs * width * length * length * 3,
+            bytes_accessed=seqs * width * length * 8,
+            transcendentals=seqs * pairs * length * length,
+        ),
+        name="attention_forward",
+    )(lens, query, key, value)
+
+
+def attention_backward_kernel(
+    lens_ref, q_ref, k_ref, v_ref, g_ref, lse_ref, dq_ref, dk_ref, dv_ref, kt_ref, dk_acc, dv_acc
+):
+    seq_len = lens_ref[pl.program_id(0)]
+    kt_ref[...] = k_ref[0].T
+    dk_acc[...] = jnp.zeros_like(dk_acc)
+    dv_acc[...] = jnp.zeros_like(dv_acc)
+    tiles = q_ref.shape[1] // TILE
+
+    def row_tile(tile):
+        rows = pl.ds(tile * TILE, TILE)
+        inner = tile * TILE
+        query = q_ref[0, rows, :] * HEAD ** (-0.5)
+        grad = g_ref[0, rows, :]
+        allowed = edge_allowed(inner, inner, seq_len)
+        spans = [(inner, TILE)] + ([(0, inner)] if inner else [])
+        outs = []
+        for half in range(2):
+            mine = one_head(query, half)
+            mine_grad = one_head(grad, half)
+            lse = lse_ref[0, 0, pl.ds(half, 1), rows]
+            probs, grad_probs, row_dot = [], [], 0.0
+            for at, (start, size) in enumerate(spans):
+                keys = pl.ds(start, size)
+                scores = lax.dot_general(
+                    k_ref[0, keys, :], mine, NT, preferred_element_type=jnp.float32
+                )
+                if at == 0:
+                    scores = jnp.where(allowed, scores, -1e30)
+                prob = jnp.exp(scores - lse)
+                dv_acc[keys, :] += jnp.dot(
+                    prob.astype(jnp.bfloat16), mine_grad, preferred_element_type=jnp.float32
+                )
+                grad_prob = lax.dot_general(
+                    v_ref[0, keys, :], mine_grad, NT, preferred_element_type=jnp.float32
+                )
+                row_dot = row_dot + jnp.sum(prob * grad_prob, axis=0, keepdims=True)
+                probs.append(prob)
+                grad_probs.append(grad_prob)
+            out = 0.0
+            for (start, size), prob, grad_prob in zip(spans, probs, grad_probs):
+                keys = pl.ds(start, size)
+                grad_scores = (prob * (grad_prob - row_dot)).astype(jnp.bfloat16)
+                dk_acc[keys, :] += jnp.dot(grad_scores, mine, preferred_element_type=jnp.float32)
+                out = out + jnp.dot(
+                    kt_ref[pl.ds(half * HEAD, HEAD), keys],
+                    grad_scores,
+                    preferred_element_type=jnp.float32,
+                )
+            outs.append(out)
+        dq = jnp.concatenate(outs, axis=0).T * HEAD ** (-0.5)
+        dq_ref[0, rows, :] = dq.astype(dq_ref.dtype)
+
+    for tile in range(tiles):
+        pl.when(tile * TILE < seq_len)(lambda tile=tile: row_tile(tile))
+
+        @pl.when(tile * TILE >= seq_len)
+        def _(tile=tile):
+            dq_ref[0, pl.ds(tile * TILE, TILE), :] = jnp.zeros((TILE, 2 * HEAD), dq_ref.dtype)
+
+    dk_ref[0] = dk_acc[...].astype(dk_ref.dtype)
+    dv_ref[0] = dv_acc[...].astype(dv_ref.dtype)
+
+
+def attention_backward(lens, query, key, value, grad, lse):
+    seqs, length, width = query.shape
+    pairs = width // (2 * HEAD)
+    spec = pl.BlockSpec((1, length, 2 * HEAD), lambda s, h, lens: (s, 0, h))
+    return pl.pallas_call(
+        attention_backward_kernel,
+        grid_spec=pltpu.PrefetchScalarGridSpec(
+            num_scalar_prefetch=1,
+            grid=(seqs, pairs),
+            in_specs=[spec] * 4
+            + [pl.BlockSpec((1, 1, 2, length), lambda s, h, lens: (s, h, 0, 0))],
+            out_specs=[spec] * 3,
+            scratch_shapes=[
+                pltpu.VMEM((2 * HEAD, length), jnp.bfloat16),
+                pltpu.VMEM((length, 2 * HEAD), jnp.float32),
+                pltpu.VMEM((length, 2 * HEAD), jnp.float32),
+            ],
+        ),
+        out_shape=[jax.ShapeDtypeStruct(query.shape, jnp.bfloat16)] * 3,
+        cost_estimate=pl.CostEstimate(
+            flops=seqs * width * length * length * 7,
+            bytes_accessed=seqs * width * length * 14,
+            transcendentals=seqs * pairs * length * length,
+        ),
+        name="attention_backward",
+    )(lens, query, key, value, grad, lse)
+
+
+def swap(value):
+    return lax.ppermute(value, "mp", [(0, 1), (1, 0)])
+
+
+def partner_shard(shard, axis):
+    size = shard.shape[axis] // 2
+    core = lax.rem(lax.axis_index("dp"), 2)
+    count = lax.axis_size("dp")
+    half = lax.dynamic_slice_in_dim(shard, core * size, size, axis)
+    mine = swap(half)
+    other = lax.ppermute(mine, "dp", [(i, i ^ 1) for i in range(count)])
+    low = jnp.where(core == 0, mine, other)
+    high = jnp.where(core == 0, other, mine)
+    return jnp.concatenate((shard, low, high), axis=axis)
+
+
+def per_device_pair(
+    tokens,
+    cotangent,
+    lengths,
+    first_norm_gain,
+    first_norm_bias,
+    query_key_value_weight,
+    attention_output_weight,
+    attention_output_bias,
+    second_norm_gain,
+    second_norm_bias,
+    feedforward_up_weight,
+    feedforward_up_bias,
+    feedforward_down_weight,
+    feedforward_down_bias,
+    adapter_down_factor,
+    adapter_up_factor,
+    down_first_moment,
+    up_first_moment,
+    down_second_moment,
+    up_second_moment,
+):
+    f32, bf16 = jnp.float32, jnp.bfloat16
+    length, width = tokens.shape[1:]
+    rank = adapter_down_factor.shape[2]
+    me = lax.axis_index("mp")
+    half_width = query_key_value_weight.shape[2]
+    whole, half = 2, length // 2
+    split = 2 * whole
+
+    def own(array, half_at):
+        entire = lax.dynamic_slice_in_dim(array, whole * me, whole, 0)
+        part = lax.dynamic_slice_in_dim(array[split], half_at * half, half, 0)
+        return jnp.concatenate((entire.reshape(whole * length, width), part), axis=0)
+
+    qkv_full = partner_shard(query_key_value_weight, 2)
+    out_full = partner_shard(attention_output_weight, 0)
+    up_full = partner_shard(feedforward_up_weight, 1)
+    up_bias = jnp.concatenate((feedforward_up_bias, swap(feedforward_up_bias)))
+    down_full = partner_shard(feedforward_down_weight, 0)
+
+    def own_first(array):
+        mine = lax.dynamic_slice_in_dim(array, me * half_width, half_width, 2)
+        theirs = lax.dynamic_slice_in_dim(array, (1 - me) * half_width, half_width, 2)
+        return mine, jnp.concatenate((mine, theirs), axis=2)
+
+    down_low = adapter_down_factor.astype(bf16)
+    down_pair = jnp.concatenate((down_low[0], down_low[1]), axis=1)
+    up_mine, up_ordered = own_first(adapter_up_factor.astype(bf16))
+
+    def dot(a, b):
+        return jnp.dot(a, b, preferred_element_type=f32)
+
+    def dot_t(a, b):
+        return lax.dot_general(a, b, NT, preferred_element_type=f32)
+
+    def project(rows, weight, up):
+        normed = layer_norm(rows.astype(f32), first_norm_gain, first_norm_bias).astype(bf16)
+        low = dot(normed, down_pair).astype(bf16)
+        query = (dot(normed, weight[0]) + 8.0 * dot(low[:, :rank], up[0])).astype(bf16)
+        key = dot(normed, weight[1]).astype(bf16)
+        value = (dot(normed, weight[2]) + 8.0 * dot(low[:, rank:], up[1])).astype(bf16)
+        return normed, low, query, key, value
+
+    own_lens = lax.dynamic_slice_in_dim(lengths, whole * me, whole, 0)
+    split_lens = lengths[split:]
+    own_tokens = own(tokens, me)
+    normed_s, low_s, query_s, key_s, value_s = project(
+        tokens[split], query_key_value_weight, up_mine
+    )
+    heads_s = [piece[None] for piece in (query_s, key_s, value_s)]
+    attended_s, lse_s = attention_forward(split_lens, *heads_s)
+    attended_s = attended_s[0]
+
+    def mine_rows(array):
+        return lax.dynamic_slice_in_dim(array, me * half, half, 0)
+
+    def theirs_rows(array):
+        return lax.dynamic_slice_in_dim(array, (1 - me) * half, half, 0)
+
+    attended_got = swap(theirs_rows(attended_s))
+    normed_w, low_w, query_w, key_w, value_w = project(
+        own_tokens[: whole * length], qkv_full, up_ordered
+    )
+    heads_w = [piece.reshape(whole, length, width) for piece in (query_w, key_w, value_w)]
+    attended_w, lse_w = attention_forward(own_lens, *heads_w)
+    attended = jnp.concatenate(
+        (
+            attended_w.reshape(whole * length, width),
+            jnp.concatenate((mine_rows(attended_s), attended_got), axis=1),
+        ),
+        axis=0,
+    )
+    tokens_f32 = own_tokens.astype(f32)
+
+    def norm_two(values):
+        return layer_norm(values, second_norm_gain, second_norm_bias)
+
+    def norm_one(values):
+        return layer_norm(values, first_norm_gain, first_norm_bias)
+
+    residual = tokens_f32 + (dot(attended, out_full) + attention_output_bias)
+    normed_two = norm_two(residual).astype(bf16)
+    hidden_pre = dot(normed_two, up_full) + up_bias
+    hidden = gelu_tanh(hidden_pre).astype(bf16)
+    block_own = (residual + dot(hidden, down_full) + feedforward_down_bias).astype(bf16)
+    block_got = swap(block_own)
+
+    def both(mine, got):
+        first = jnp.where(me == 0, mine, got)
+        second = jnp.where(me == 0, got, mine)
+        parts = (
+            first[: whole * length],
+            second[: whole * length],
+            first[whole * length :],
+            second[whole * length :],
+        )
+        return jnp.concatenate(parts, axis=0).reshape(tokens.shape)
+
+    block_out = both(block_own, block_got)
+    at = jnp.arange(length)
+    live = jnp.concatenate(
+        (
+            (at[None, :] < own_lens[:, None]).reshape(-1, 1),
+            (mine_rows(at) < split_lens[0]).reshape(-1, 1),
+        ),
+        axis=0,
+    )
+    grad_out = jnp.where(live, own(cotangent, me), jnp.zeros((), bf16))
+    grad_hidden = dot_t(grad_out, down_full)
+    _, gelu_back = jax.vjp(gelu_tanh, hidden_pre)
+    grad_pre = gelu_back(grad_hidden)[0].astype(bf16)
+    grad_norm2 = dot_t(grad_pre, up_full)
+    _, norm2_back = jax.vjp(norm_two, residual)
+    grad_resid = grad_out.astype(f32) + norm2_back(grad_norm2)[0]
+    grad_attended = dot_t(grad_resid.astype(bf16), out_full).astype(bf16)
+    grad_got = swap(grad_attended[whole * length :, half_width:])
+    grad_kept = grad_attended[whole * length :, :half_width]
+    grad_s = jnp.concatenate(
+        (
+            jnp.where(me == 0, grad_kept, grad_got),
+            jnp.where(me == 0, grad_got, grad_kept),
+        ),
+        axis=0,
+    )
+    grads_s = attention_backward(split_lens, *heads_s, grad_s[None], lse_s)
+    grads_w = attention_backward(
+        own_lens,
+        *heads_w,
+        grad_attended[: whole * length].reshape(whole, length, width),
+        lse_w,
+    )
+    pack_s = jnp.stack([piece[0] for piece in grads_s])
+    sent = swap(lax.dynamic_slice_in_dim(pack_s, (1 - me) * half, half, 1))
+    kept = lax.dynamic_slice_in_dim(pack_s, me * half, half, 1)
+    tail = jnp.concatenate((kept, sent), axis=2)
+    grad_query, grad_key, grad_value = (
+        jnp.concatenate((grads_w[i].reshape(whole * length, width), tail[i]), axis=0)
+        for i in range(3)
+    )
+    adapter_gradient = 8.0 * jnp.concatenate(
+        (dot_t(grad_query, up_ordered[0]), dot_t(grad_value, up_ordered[1])), axis=1
+    )
+    grad_norm1 = (
+        dot_t(grad_query, qkv_full[0])
+        + dot_t(grad_key, qkv_full[1])
+        + dot_t(grad_value, qkv_full[2])
+        + jnp.einsum(
+            "gy,wy->gw", adapter_gradient, down_pair.astype(f32), precision=lax.Precision.HIGHEST
+        )
+    )
+    _, norm1_back = jax.vjp(norm_one, tokens_f32)
+    input_own = (grad_resid + norm1_back(grad_norm1)[0]).astype(bf16)
+    input_grad = both(input_own, swap(input_own))
+
+    normed = jnp.concatenate((normed_w, mine_rows(normed_s)), axis=0)
+    low = jnp.concatenate((low_w, mine_rows(low_s)), axis=0)
+    grad_down_both = jnp.einsum(
+        "fi,fg->ig", normed.astype(f32), adapter_gradient, precision=lax.Precision.HIGHEST
+    )
+    grad_down = jnp.stack((grad_down_both[:, :rank], grad_down_both[:, rank:]))
+    grad_up = 8.0 * jnp.stack(
+        (
+            jnp.einsum("zm,zj->mj", low[:, :rank], grad_query, preferred_element_type=f32),
+            jnp.einsum("zm,zj->mj", low[:, rank:], grad_value, preferred_element_type=f32),
+        )
+    )
+    first = jnp.where(me == 0, grad_up[:, :, :half_width], grad_up[:, :, half_width:])
+    second = jnp.where(me == 0, grad_up[:, :, half_width:], grad_up[:, :, :half_width])
+    grad_up = jnp.concatenate((first, second), axis=2)
+    live_local = jnp.sum(lengths).astype(f32)
+    down_sum, up_sum, live_sum = lax.psum((grad_down, grad_up, live_local), ("dp", "mp"))
+    active = live_sum / 2
+    new_down = adam_decay_update(
+        adapter_down_factor, down_sum / active, down_first_moment, down_second_moment
+    )
+    new_up = adam_decay_update(
+        adapter_up_factor, up_sum / active, up_first_moment, up_second_moment
+    )
+    return (
+        block_out,
+        input_grad,
+        new_down[0],
+        new_up[0],
+        new_down[1],
+        new_up[1],
+        new_down[2],
+        new_up[2],
+    )
+
+
 def solution(mesh):
     in_specs = (
         P("dp", None, None),
@@ -324,5 +741,9 @@
     )
     out_specs = (P("dp", None, None), P("dp", None, None), P(), P(), P(), P(), P(), P())
     return jax.shard_map(
-        per_device, mesh=mesh, in_specs=in_specs, out_specs=out_specs, check_vma=False
-    )
+        per_device_pair if mesh.shape["mp"] == 2 else per_device,
+        mesh=mesh,
+        in_specs=in_specs,
+        out_specs=out_specs,
+        check_vma=False,
+    )

time: 3260 us -> 928 us (0.28)
  waiting for transfers between devices: 1570 us -> 35 us
  matrix products: 911 us -> 303 us
  local copies, waits for them, and re-layouts: 344 us -> 105 us
  other arithmetic: 344 us -> 113 us
  Pallas kernels: 0 us -> 126 us
  blocking collectives: 41.1 us -> 161 us
  starting transfers between devices: 0.33 us -> 65.9 us
    reduce_scatter x4 -> x0, waiting for transfers between devices: 791 us -> none  [the longest x1 234 us: per_device(): lax.psum_scatter(partial_sum + jnp.einsum('gy,wy->gw', adapter_gradient,...]
    all_gather x4 -> x0, waiting for transfers between devices: 783 us -> none  [the longest x1 242 us: per_device(): grad_norm2 = lax.all_gather(grad_norm2_share, 'mp', axis=0, tiled=True)]
    dot_general x301 -> x27, matrix products: 911 us -> 303 us  [the longest x8 153 us: dot_t(): return lax.dot_general(a, b, NT, preferred_element_type=f32)]
    pallas_call x0 -> x4, Pallas kernels: none -> 126 us  [the longest x2 76.5 us: attention_forward(): pl.pallas_call(attention_forward_kernel, grid_spec=pltpu.PrefetchScalarGr...]
    psum x1, blocking collectives: 41.1 us -> 161 us  [per_device_pair(): lax.psum((grad_down, grad_up, live_local), ('dp', 'mp'))]
    reduce_sum x43 -> x1, other arithmetic: 108 us -> 0.63 us  [per_device_pair(): live_local = jnp.sum(lengths).astype(f32)]
    reshape x9 -> x3, local copies, waits for them, and re-layouts: 111 us -> 13.1 us  [the longest x2 13.1 us: own(): entire.reshape(whole * length, width)]
    convert_element_type x45 -> x7, other arithmetic: 93.9 us -> 17.9 us  [the longest x1 9.49 us: per_device_pair(): input_own = (grad_resid + norm1_back(grad_norm1)[0]).astype(bf16)]
  transfers between devices with their start and end apart: 8 -> 14, of which waited for: 8 -> 2; matrix products, arithmetic and copies ran while one was open for 3% -> 35% of each run, Pallas kernels for 0% -> 12%
where the time goes in v1:
time: 928 us; the launch traced here: 913 us
  matrix products  303 us (33%)
  blocking collectives  161 us (17%)
  Pallas kernels  126 us (14%)
  other arithmetic  113 us (12%)
  local copies, waits for them, and re-layouts  105 us (11%)
  starting transfers between devices  65.9 us (7%)
  waiting for transfers between devices  35 us (4%)
    psum x1, blocking collectives, per_device_pair(): lax.psum((grad_down, grad_up, live_local), ('dp', 'mp'))  161 us
    dot_general x8, matrix products, dot_t(): return lax.dot_general(a, b, NT, preferred_element_type=f32)  153 us
    dot_general x15, matrix products, dot(): return jnp.dot(a, b, preferred_element_type=f32)  125 us
    pallas_call x2, Pallas kernels, attention_forward(): pl.pallas_call(attention_forward_kernel, grid_spec=pltpu.PrefetchScalarGr...  76.5 us
    ppermute x10, starting transfers between devices, swap(): return lax.ppermute(value, 'mp', [(0, 1), (1, 0)])  59.8 us
    pallas_call x2, Pallas kernels, attention_backward(): pl.pallas_call(attention_backward_kernel, grid_spec=pltpu.PrefetchScalarG...  49.4 us
    ppermute x10, waiting for transfers between devices, swap(): return lax.ppermute(value, 'mp', [(0, 1), (1, 0)])  34.9 us
    concatenate x2, local copies, waits for them, and re-layouts, both(): return jnp.concatenate(parts, axis=0).reshape(tokens.shape)  28.8 us
  transfers between devices with their start and end apart: 14, of which 2 were waited for; matrix products, arithmetic and copies ran while one was open for 35% of the time, Pallas kernels for 12%

profile of v1, /device:TPU:31, one launch (start us, length us, event | category | flops | bytes accessed | tf_op | source)
XLA Modules:
  0.0 913.1 jit_solution(14093515235861650417)
XLA Ops:
  39.9 6.5 copy.43
  73.0 17.6 %attention_forward.3 = (bf16[1,1024,512]{2,1,0:T(8,128)(2,1)}, f32[1,4,2,1024]{3,2,1,0:T(2,128)}) custom-call(s32[1]{0:T(128)} %slice.135.lens_ref, bf16[1,1024,512]{2,1,0:T(8,128)(2,1)} %fusion.60.q_ref, bf16[1,1024,512]{2,1,0:T(8,128)(2,1)} %fusion.59.k_ref, bf16[1,1024,512]{2,1,0:T(8,128)(2,1)} %fusion.61.v_ref), custom_call_target="tpu_custom_call" | custom-call | flops 1610612736 | bytes 4194304 | tf_op jit(solution)/shard_map/attention_forward/pallas_call | solution.py:378
  99.5 6.5 copy.44
  109.6 29.7 %collective-permute-done.5 = bf16[1024,1024]{1,0:T(8,128)(2,1)} collective-permute-done((bf16[1024,1024]{1,0:T(8,128)(2,1)}, bf16[1024,1024]{1,0:T(8,128)(2,1)}, u32[]{:S(2)}, u32[]{:S(2)}) %collective-permute-start.5) | collective-permute-done | bytes 2097184 | tf_op jit(solution)/shard_map/ppermute | solution.py:493
  153.5 8.5 add_convert_fusion.3
  162.1 8.3 add_convert_fusion.4
  170.4 59.0 %attention_forward.2 = (bf16[2,1024,1024]{2,1,0:T(8,128)(2,1)}, f32[2,8,2,1024]{3,2,1,0:T(2,128)}) custom-call(s32[2]{0:T(128)} %copy-done.61, bf16[2,1024,1024]{2,1,0:T(8,128)(2,1)} %bitcast.149, bf16[2,1024,1024]{2,1,0:T(8,128)(2,1)} %bitcast.145, bf16[2,1024,1024]{2,1,0:T(8,128)(2,1)} %bitcast.147), custom_call_target="tpu_custom_call" | custom-call | flops 6442450944 | bytes 16777216 | tf_op jit(solution)/shard_map/attention_forward/pallas_call | solution.py:378
  229.4 15.6 %fusion.140 = (f32[2560]{0:T(1024)S(1)}, f32[2560,1024]{0,1:T(8,128)}) fusion(f32[1024]{0:T(1024)S(1)} %copy-done.62, bf16[256,1024]{1,0:T(8,128)(2,1)S(1)} %get-tuple-element.69, bf16[256,1024]{1,0:T(8,128)(2,1)S(1)} %get-tuple-element.68, bf16[512,1024]{1,0:T(8,128)(2,1)} %param.26, bf16[512,512]{1,0:T(8,128)(2,1)} %collective-permute-done.2, ...), kind=kOutput, calls=%fused_computation.257 | convolution fusion | flops 5409076736 | bytes 23083008 | tf_op jit(solution)/shard_map/dot_general | solution.py:559
  255.8 34.7 %fusion.21 = f32[2560,4096]{1,0:T(8,128)} fusion(f32[2560,1024]{0,1:T(8,128)} %get-tuple-element.87, f32[1024]{0:T(1024)S(1)} %copy-done.63, f32[1024]{0:T(1024)S(1)} %copy-done.60, f32[2560]{0:T(1024)S(1)} %fusion.88, f32[2560]{0:T(1024)S(1)} %broadcast_multiply_fusion.1, bf16[1024,1024]{1,0:T(8,128)(2,1)} %get-tuple-element.60, ...), kind=kOutput, calls=%fused_computation.51 | convolution fusion | flops 21513109504 | bytes 60846080 | tf_op jit(solution)/shard_map/dot_general | solution.py:559
  296.0 77.5 %fusion.3.clone.1.clone.5 = bf16[2560,4096]{1,0:T(8,128)(2,1)} fusion(f32[2560,4096]{1,0:T(8,128)} %fusion.21, f32[4096]{0:T(1024)S(1)} %pad_maximum_fusion.32, bf16[1024,1024]{1,0:T(8,128)(2,1)S(1)} %get-tuple-element.58, bf16[1024,1024]{1,0:T(8,128)(2,1)S(1)} %get-tuple-element.57, bf16[2048,1024]{1,0:T(8,128)(2,1)S(1)} %copy-done.12, ...), kind=kOutput, calls=%fused_computation.7.clone.clone.clone.clone.clone.2 | convolution fusion | flops 21775253504 | bytes 76564992 | tf_op jit(solution)/shard_map/dot_general | solution.py:562
  373.5 33.3 %multiply_reduce_fusion = (f32[2560]{0:T(1024)S(1)}, f32[2560,1024]{0,1:T(8,128)}) fusion(f32[2560,1024]{0,1:T(8,128)} %get-tuple-element.87, f32[1024]{0:T(1024)S(1)} %copy-done.60, f32[2560]{0:T(1024)S(1)} %broadcast_multiply_fusion.1, bf16[1024,1024]{1,0:T(8,128)(2,1)} %get-tuple-element.60, bf16[1024,1024]{1,0:T(8,128)(2,1)} %copy-done.21, ...), kind=kOutput, calls=%fused_computation.30 | convolution fusion | flops 21510486016 | bytes 50356224 | tf_op jit(solution)/shard_map/dot_general | solution.py:562
  406.7 13.0 %fusion.139 = (f32[2560]{0:T(1024)S(1)}, f32[2560,1024]{0,1:T(8,128)}) fusion(f32[2560]{0:T(1024)S(1)} %multiply_multiply_fusion.5, f32[2560,1024]{0,1:T(8,128)} %get-tuple-element.87, f32[2560]{0:T(1024)S(1)} %broadcast_multiply_fusion.1, f32[2560]{0:T(1024)S(1)} %fusion.88, f32[2560,1024]{0,1:T(8,128)} %get-tuple-element.89, f32[1024]{0:T(1024)S(1)} %copy-done.60), kind=kLoop, calls=%fused_computation.256 | loop fusion | flops 18347520 | bytes 31502336 | tf_op jit(solution)/shard_map/transpose(jvp())/reduce_sum | solution.py:12
  419.8 13.0 %convolution_convert_fusion = bf16[2560,1024]{1,0:T(8,128)(2,1)} fusion(f32[2560,1024]{0,1:T(8,128)} %get-tuple-element.48, f32[2560]{0:T(1024)S(1)} %negate_multiply_fusion.1, bf16[256,1024]{1,0:T(8,128)(2,1)} %copy-done.29, bf16[256,1024]{1,0:T(8,128)(2,1)} %copy-done.28, bf16[512,1024]{1,0:T(8,128)(2,1)} %param.26, bf16[512,1024]{0,1:T(8,128)(2,1)} %bitcast.141, ...), kind=kOutput, calls=%fused_computation.50 | convolution fusion | flops 5401214976 | bytes 23081472 | tf_op jit(solution)/shard_map/dot_general | solution.py:562
  433.8 10.2 %collective-permute-start.11 = (bf16[512,512]{1,0:T(8,128)(2,1)S(1)}, bf16[512,512]{1,0:T(8,128)(2,1)S(1)}, u32[]{:S(2)}, u32[]{:S(2)}) collective-permute-start(bf16[512,512]{1,0:T(8,128)(2,1)S(1)} %slice.181), channel_id=1, source_target_pairs={{0,1},{1,0},{2,3},{3,2},{4,5},{5,4},{6,7},{7,6},{8,9},{9,8},{10,11... | collective-permute-start | bytes 1572872 | tf_op jit(solution)/shard_map/ppermute | solution.py:493
  444.0 6.5 pad_maximum_fusion.46
  458.0 13.7 %attention_backward.3 = (bf16[1,1024,512]{2,1,0:T(8,128)(2,1)}, bf16[1,1024,512]{2,1,0:T(8,128)(2,1)}, bf16[1,1024,512]{2,1,0:T(8,128)(2,1)}) custom-call(s32[1]{0:T(128)} %slice.135.lens_ref, bf16[1,1024,512]{2,1,0:T(8,128)(2,1)} %fusion.60.q_ref, bf16[1,1024,512]{2,1,0:T(8,128)(2,1)} %fusion.59.k_ref, bf16[1,1024,512]{2,1,0:T(8,128)(2,1)} %fusion.61.v_ref, ...), custom_call_target="tpu_custom_call" | custom-call | flops 3758096384 | bytes 7340032 | tf_op jit(solution)/shard_map/attention_backward/pallas_call | solution.py:468
  478.7 31.3 %add_convert_fusion.1 = bf16[2560,1024]{0,1:T(8,128)(2,1)} fusion(f32[2560,1024]{0,1:T(8,128)} %get-tuple-element.87, f32[2560,4096]{1,0:T(8,128)} %fusion.21, f32[4096]{0:T(1024)S(1)} %pad_maximum_fusion.32, f32[1024]{0:T(1024)S(1)} %copy-done.64, bf16[4096,1024]{1,0:T(8,128)(2,1)} %pad_maximum_fusion.46), kind=kOutput, calls=%fused_computation.31 | convolution fusion | flops 21587558400 | bytes 66080768 | tf_op jit(solution)/shard_map/dot_general | solution.py:559
  514.7 35.6 %attention_backward.2 = (bf16[2,1024,1024]{2,1,0:T(8,128)(2,1)}, bf16[2,1024,1024]{2,1,0:T(8,128)(2,1)}, bf16[2,1024,1024]{2,1,0:T(8,128)(2,1)}) custom-call(s32[2]{0:T(128)} %copy-done.61, bf16[2,1024,1024]{2,1,0:T(8,128)(2,1)} %bitcast.150, bf16[2,1024,1024]{2,1,0:T(8,128)(2,1)} %bitcast.146, bf16[2,1024,1024]{2,1,0:T(8,128)(2,1)} %bitcast.148, ...), custom_call_target="tpu_custom_call" | custom-call | flops 15032385536 | bytes 29360128 | tf_op jit(solution)/shard_map/attention_backward/pallas_call | solution.py:468
  555.4 8.7 fusion.54
  565.6 8.7 fusion.53
  574.4 8.7 fusion.27
  583.1 17.0 %fusion.11 = (f32[2560]{0:T(1024)S(1)}, f32[2560]{0:T(1024)S(1)}, f32[2560,1024]{0,1:T(8,128)}) fusion(f32[2560]{0:T(1024)S(1)} %copy-done.33, bf16[512,1024]{0,1:T(8,128)(2,1)} %copy-done.5, bf16[2048,1024]{0,1:T(8,128)(2,1)S(1)} %copy-done.1, f32[1024]{0:T(1024)S(1)} %copy-done.45, bf16[1024,4]{0,1:T(4,128)(2,1)S(1)} %copy-done.41, ...), kind=kOutput, calls=%fused_computation.23 | convolution fusion | flops 285805568 | bytes 47319040 | tf_op jit(solution)/shard_map/gy,wy->gw/dot_general | solution.py:675
  600.2 7.2 fusion.40
  609.1 9.5 %add_convert_fusion = bf16[2560,1024]{0,1:T(8,128)(2,1)} fusion(f32[2560,1024]{0,1:T(8,128)} %get-tuple-element.48, f32[2560]{0:T(1024)S(1)} %negate_multiply_fusion, f32[2560]{0:T(1024)S(1)} %copy-done.52, f32[2560]{0:T(1024)S(1)} %get-tuple-element.81, f32[2560]{0:T(1024)S(1)} %copy-done.33, f32[2560,1024]{0,1:T(8,128)S(1)} %copy-done.2, ...), kind=kLoop, calls=%fused_computation.27 | loop fusion | flops 52428800 | bytes 36753920 | tf_op jit(solution)/shard_map/convert_element_type | solution.py:680
  618.6 43.3 %collective-permute-start.13 = (bf16[2560,1024]{0,1:T(8,128)(2,1)}, bf16[2560,1024]{0,1:T(8,128)(2,1)}, u32[]{:S(2)}, u32[]{:S(2)}) collective-permute-start(bf16[2560,1024]{0,1:T(8,128)(2,1)} %add_convert_fusion), channel_id=1, source_target_pairs={{0,1},{1,0},{2,3},{3,2},{4,5},{5,4},{6,7},{7,6},{8,9},{9,8},{10,11... | collective-permute-start | bytes 15728648 | tf_op jit(solution)/shard_map/ppermute | solution.py:493
  674.5 161.2 %all-reduce.2 = (f32[2,1024,4]{1,2,0:T(4,128)S(1)}, f32[]{:T(128)}, f32[2,4,1024]{2,1,0:T(4,128)S(1)}) all-reduce(f32[2,1024,4]{1,2,0:T(4,128)S(1)} %pad_maximum_fusion.27, f32[]{:T(128)S(6)} %convert_element_type.130, f32[2,4,1024]{2,1,0:T(4,128)S(1)} %pad_maximum_fusion.28), channel_id=1, replica_groups=mesh['dp'=16,'mp'=2] {'dp','mp'}, use_global_device_ids=true, to_apply=%region_12.13 | all-reduce | flops 16385 | bytes 131080 | tf_op jit(solution)/shard_map/psum | solution.py:699
  837.8 8.8 broadcast_select_fusion.3
  851.6 9.3 %pad_maximum_fusion = bf16[5120,1024]{0,1:T(8,128)(2,1)} fusion(bf16[512,1024]{0,1:T(8,128)(2,1)S(1)} %slice.178, bf16[512,1024]{0,1:T(8,128)(2,1)S(1)} %slice.177, bf16[2048,1024]{0,1:T(8,128)(2,1)S(1)} %slice.176, bf16[2048,1024]{0,1:T(8,128)(2,1)S(1)} %slice.175), kind=kLoop, calls=%fused_computation.25 | loop fusion | flops 41943040 | bytes 20971520 | tf_op jit(solution)/shard_map/concatenate | solution.py:625
  860.9 14.4 %copy.38 = bf16[5120,1024]{1,0:T(8,128)(2,1)} copy(bf16[5120,1024]{0,1:T(8,128)(2,1)} %pad_maximum_fusion) | data formatting | bytes 20971520 | tf_op jit(solution)/shard_map/concatenate | solution.py:625
  875.3 8.8 broadcast_select_fusion.1
  889.1 9.4 %pad_maximum_fusion.1 = bf16[5120,1024]{0,1:T(8,128)(2,1)} fusion(bf16[512,1024]{0,1:T(8,128)(2,1)S(1)} %slice.189, bf16[512,1024]{0,1:T(8,128)(2,1)S(1)} %slice.188, bf16[2048,1024]{0,1:T(8,128)(2,1)S(1)} %slice.187, bf16[2048,1024]{0,1:T(8,128)(2,1)S(1)} %slice.186), kind=kLoop, calls=%fused_computation.26 | loop fusion | flops 41943040 | bytes 20971520 | tf_op jit(solution)/shard_map/concatenate | solution.py:625
  898.5 14.4 %copy.41 = bf16[5120,1024]{1,0:T(8,128)(2,1)} copy(bf16[5120,1024]{0,1:T(8,128)(2,1)} %pad_maximum_fusion.1) | data formatting | bytes 20971520 | tf_op jit(solution)/shard_map/concatenate | solution.py:625
  (287 shorter events, 159.9 us)
Async XLA Ops:
  0.6 105.4 %collective-permute-start.7 = (f32[2048]{0:T(1024)}, f32[2048]{0:T(1024)S(1)}, u32[]{:S(2)}, u32[]{:S(2)}) collective-permute-start(f32[2048]{0:T(1024)} %param.31), channel_id=1, source_target_pairs={{0,1},{1,0},{2,3},{3,2},{4,5},{5,4},{6,7},{7,6},{8,9},{9,8},{10,11... | collective-permute-start | bytes 24584 | tf_op jit(solution)/shard_map/ppermute | solution.py:493
  2.8 93.7 %collective-permute-start.3 = (bf16[256,1024]{1,0:T(8,128)(2,1)}, bf16[256,1024]{1,0:T(8,128)(2,1)}, u32[]{:S(2)}, u32[]{:S(2)}) collective-permute-start(bf16[256,1024]{1,0:T(8,128)(2,1)} %constant_dynamic-slice_fusion.10), channel_id=1, source_target_pairs={{0,1},{1,0},{2,3},{3,2},{4,5},{5,4},{6,7},{7,6},{8,9},{9,8},{10,11... | collective-permute-start | bytes 1572872 | tf_op jit(solution)/shard_map/ppermute | solution.py:493
  6.8 64.1 %collective-permute-start = (bf16[3,1024,256]{2,1,0:T(8,128)(2,1)}, bf16[3,1024,256]{2,1,0:T(8,128)(2,1)}, u32[]{:S(2)}, u32[]{:S(2)}) collective-permute-start(bf16[3,1024,256]{2,1,0:T(8,128)(2,1)} %constant_dynamic-slice_fusion.13), channel_id=1, source_target_pairs={{0,1},{1,0},{2,3},{3,2},{4,5},{5,4},{6,7},{7,6},{8,9},{9,8},{10,11... | collective-permute-start | bytes 4718600 | tf_op jit(solution)/shard_map/ppermute | solution.py:493
  10.3 98.4 %collective-permute-start.8 = (bf16[1024,1024]{1,0:T(8,128)(2,1)}, bf16[1024,1024]{1,0:T(8,128)(2,1)}, u32[]{:S(2)}, u32[]{:S(2)}) collective-permute-start(bf16[1024,1024]{1,0:T(8,128)(2,1)} %constant_dynamic-slice_fusion.8), channel_id=1, source_target_pairs={{0,1},{1,0},{2,3},{3,2},{4,5},{5,4},{6,7},{7,6},{8,9},{9,8},{10,11... | collective-permute-start | bytes 6291464 | tf_op jit(solution)/shard_map/ppermute | solution.py:493
  13.1 126.1 %collective-permute-start.5 = (bf16[1024,1024]{1,0:T(8,128)(2,1)}, bf16[1024,1024]{1,0:T(8,128)(2,1)}, u32[]{:S(2)}, u32[]{:S(2)}) collective-permute-start(bf16[1024,1024]{1,0:T(8,128)(2,1)} %constant_dynamic-slice_fusion.9), channel_id=1, source_target_pairs={{0,1},{1,0},{2,3},{3,2},{4,5},{5,4},{6,7},{7,6},{8,9},{9,8},{10,11... | collective-permute-start | bytes 6291464 | tf_op jit(solution)/shard_map/ppermute | solution.py:493
  33.4 196.0 %copy-start.5 = (bf16[512,1024]{0,1:T(8,128)(2,1)}, bf16[512,1024]{0,1:T(8,128)(2,1)S(1)}, u32[]{:S(2)}) copy-start(bf16[512,1024]{0,1:T(8,128)(2,1)S(1)} %dynamic-slice_bitcast_fusion) | copy-start | bytes 3145732
  70.9 71.5 %collective-permute-start.1 = (bf16[3,1024,256]{2,1,0:T(8,128)(2,1)}, bf16[3,1024,256]{2,1,0:T(8,128)(2,1)}, u32[]{:S(2)}, u32[]{:S(2)}) collective-permute-start(bf16[3,1024,256]{2,1,0:T(8,128)(2,1)} %collective-permute-done), channel_id=1, source_target_pairs={{0,2},{2,0},{4,6},{6,4},{8,10},{10,8},{12,14},{14,12},{16,18},{18,... | collective-permute-start | bytes 4718600 | tf_op jit(solution)/shard_map/ppermute | solution.py:502
  96.5 10.9 %collective-permute-start.4 = (bf16[256,1024]{1,0:T(8,128)(2,1)}, bf16[256,1024]{1,0:T(8,128)(2,1)}, u32[]{:S(2)}, u32[]{:S(2)}) collective-permute-start(bf16[256,1024]{1,0:T(8,128)(2,1)} %collective-permute-done.3), channel_id=1, source_target_pairs={{0,2},{2,0},{4,6},{6,4},{8,10},{10,8},{12,14},{14,12},{16,18},{18,... | collective-permute-start | bytes 1572872 | tf_op jit(solution)/shard_map/ppermute | solution.py:502
  106.0 38.5 %copy-start.15 = (bf16[3,1024,512]{2,1,0:T(8,128)(2,1)S(1)}, bf16[3,1024,512]{2,1,0:T(8,128)(2,1)}, u32[]{:S(2)}) copy-start(bf16[3,1024,512]{2,1,0:T(8,128)(2,1)} %param.25) | copy-start | bytes 9437188
  106.1 313.7 %copy-start.57 = (pred[2560]{0:T(1024)(128)(4,1)}, pred[2560]{0:T(1024)(128)(4,1)S(1)}, u32[]{:S(2)}) copy-start(pred[2560]{0:T(1024)(128)(4,1)S(1)} %add_reduce_fusion) | copy-start | bytes 7684
  106.1 123.3 %collective-permute-start.2 = (bf16[512,512]{1,0:T(8,128)(2,1)}, bf16[512,512]{1,0:T(8,128)(2,1)}, u32[]{:S(2)}, u32[]{:S(2)}) collective-permute-start(bf16[512,512]{1,0:T(8,128)(2,1)} %get-tuple-element.71), channel_id=1, source_target_pairs={{0,1},{1,0},{2,3},{3,2},{4,5},{5,4},{6,7},{7,6},{8,9},{9,8},{10,11... | collective-permute-start | bytes 1572872 | tf_op jit(solution)/shard_map/ppermute | solution.py:493
  108.7 120.7 %copy-start.28 = (bf16[256,1024]{1,0:T(8,128)(2,1)}, bf16[256,1024]{1,0:T(8,128)(2,1)S(1)}, u32[]{:S(2)}) copy-start(bf16[256,1024]{1,0:T(8,128)(2,1)S(1)} %get-tuple-element.68) | copy-start | bytes 1572868
  108.7 120.7 %copy-start.29 = (bf16[256,1024]{1,0:T(8,128)(2,1)}, bf16[256,1024]{1,0:T(8,128)(2,1)S(1)}, u32[]{:S(2)}) copy-start(bf16[256,1024]{1,0:T(8,128)(2,1)S(1)} %get-tuple-element.69) | copy-start | bytes 1572868
  108.7 181.8 %collective-permute-start.9 = (bf16[1024,1024]{1,0:T(8,128)(2,1)}, bf16[1024,1024]{1,0:T(8,128)(2,1)}, u32[]{:S(2)}, u32[]{:S(2)}) collective-permute-start(bf16[1024,1024]{1,0:T(8,128)(2,1)} %collective-permute-done.8), channel_id=1, source_target_pairs={{0,2},{2,0},{4,6},{6,4},{8,10},{10,8},{12,14},{14,12},{16,18},{18,... | collective-permute-start | bytes 6291464 | tf_op jit(solution)/shard_map/ppermute | solution.py:502
  139.2 111.5 %collective-permute-start.6 = (bf16[1024,1024]{1,0:T(8,128)(2,1)}, bf16[1024,1024]{1,0:T(8,128)(2,1)}, u32[]{:S(2)}, u32[]{:S(2)}) collective-permute-start(bf16[1024,1024]{1,0:T(8,128)(2,1)} %collective-permute-done.5), channel_id=1, source_target_pairs={{0,2},{2,0},{4,6},{6,4},{8,10},{10,8},{12,14},{14,12},{16,18},{18,... | collective-permute-start | bytes 6291464 | tf_op jit(solution)/shard_map/ppermute | solution.py:502
  170.4 59.0 %copy-start.30 = (bf16[512,512]{1,0:T(8,128)(2,1)S(1)}, bf16[512,512]{1,0:T(8,128)(2,1)}, u32[]{:S(2)}) copy-start(bf16[512,512]{1,0:T(8,128)(2,1)} %get-tuple-element.70) | copy-start | bytes 1572868
  170.4 59.0 %copy-start.62 = (f32[1024]{0:T(1024)S(1)}, f32[1024]{0:T(1024)}, u32[]{:S(2)}) copy-start(f32[1024]{0:T(1024)} %param.27) | copy-start | bytes 12292
  373.5 33.3 %copy-start.43 = (f32[2560]{0:T(1024)S(1)}, f32[2560]{0:T(1024)}, u32[]{:S(2)}) copy-start(f32[2560]{0:T(1024)} %copy-done.42) | copy-start | bytes 30724
  433.8 22.0 %collective-permute-start.11 = (bf16[512,512]{1,0:T(8,128)(2,1)S(1)}, bf16[512,512]{1,0:T(8,128)(2,1)S(1)}, u32[]{:S(2)}, u32[]{:S(2)}) collective-permute-start(bf16[512,512]{1,0:T(8,128)(2,1)S(1)} %slice.181), channel_id=1, source_target_pairs={{0,1},{1,0},{2,3},{3,2},{4,5},{5,4},{6,7},{7,6},{8,9},{9,8},{10,11... | collective-permute-start | bytes 1572872 | tf_op jit(solution)/shard_map/ppermute | solution.py:493
  477.1 73.3 %collective-permute-start.12 = (bf16[3,512,512]{2,1,0:T(8,128)(2,1)}, bf16[3,512,512]{2,1,0:T(8,128)(2,1)S(1)}, u32[]{:S(2)}, u32[]{:S(2)}) collective-permute-start(bf16[3,512,512]{2,1,0:T(8,128)(2,1)} %get-tuple-element.65), channel_id=1, source_target_pairs={{0,1},{1,0},{2,3},{3,2},{4,5},{5,4},{6,7},{7,6},{8,9},{9,8},{10,11... | collective-permute-start | bytes 4718600 | tf_op jit(solution)/shard_map/ppermute | solution.py:493
  514.7 323.1 %collective-permute-start.10 = (bf16[2560,1024]{0,1:T(8,128)(2,1)}, bf16[2560,1024]{0,1:T(8,128)(2,1)}, u32[]{:S(2)}, u32[]{:S(2)}) collective-permute-start(bf16[2560,1024]{0,1:T(8,128)(2,1)} %add_convert_fusion.1), channel_id=1, source_target_pairs={{0,1},{1,0},{2,3},{3,2},{4,5},{5,4},{6,7},{7,6},{8,9},{9,8},{10,11... | collective-permute-start | bytes 15728648 | tf_op jit(solution)/shard_map/ppermute | solution.py:493
  609.0 52.9 %copy-start.66 = (s32[5]{0:T(128)S(1)}, s32[5]{0:T(128)}, u32[]{:S(2)}) copy-start(s32[5]{0:T(128)} %param.22) | copy-start | bytes 64
  609.1 54.1 %copy-start.32 = (bf16[1024,8]{0,1:T(8,128)(2,1)S(1)}, bf16[1024,8]{0,1:T(8,128)(2,1)}, u32[]{:S(2)}) copy-start(bf16[1024,8]{0,1:T(8,128)(2,1)} %copy-done.31) | copy-start | bytes 49156
  609.1 55.6 %copy-start.27 = (bf16[2048,8]{0,1:T(8,128)(2,1)S(1)}, bf16[2048,8]{0,1:T(8,128)(2,1)}, u32[]{:S(2)}) copy-start(bf16[2048,8]{0,1:T(8,128)(2,1)} %copy-done.26) | copy-start | bytes 98308
  618.6 49.5 %copy-start.24 = (bf16[512,1024]{1,0:T(8,128)(2,1)S(1)}, bf16[512,1024]{1,0:T(8,128)(2,1)}, u32[]{:S(2)}) copy-start(bf16[512,1024]{1,0:T(8,128)(2,1)} %copy-done.23) | copy-start | bytes 3145732
  618.6 256.7 %collective-permute-start.13 = (bf16[2560,1024]{0,1:T(8,128)(2,1)}, bf16[2560,1024]{0,1:T(8,128)(2,1)}, u32[]{:S(2)}, u32[]{:S(2)}) collective-permute-start(bf16[2560,1024]{0,1:T(8,128)(2,1)} %add_convert_fusion), channel_id=1, source_target_pairs={{0,1},{1,0},{2,3},{3,2},{4,5},{5,4},{6,7},{7,6},{8,9},{9,8},{10,11... | collective-permute-start | bytes 15728648 | tf_op jit(solution)/shard_map/ppermute | solution.py:493
  668.9 167.5 %copy-start.35 = (f32[2,1024,4]{1,2,0:T(4,128)S(1)}, f32[2,1024,4]{1,2,0:T(4,128)}, u32[]{:S(2)}) copy-start(f32[2,1024,4]{1,2,0:T(4,128)} %param.34) | copy-start | bytes 98308
  668.9 167.5 %copy-start.53 = (f32[2,1024,4]{1,2,0:T(4,128)S(1)}, f32[2,1024,4]{1,2,0:T(4,128)}, u32[]{:S(2)}) copy-start(f32[2,1024,4]{1,2,0:T(4,128)} %param.36) | copy-start | bytes 98308
  668.9 167.5 %copy-start.54 = (f32[2,1024,4]{1,2,0:T(4,128)S(1)}, f32[2,1024,4]{1,2,0:T(4,128)}, u32[]{:S(2)}) copy-start(f32[2,1024,4]{1,2,0:T(4,128)} %param.38) | copy-start | bytes 98308
  668.9 168.2 %copy-start.37 = (f32[2,4,1024]{2,1,0:T(4,128)S(1)}, f32[2,4,1024]{2,1,0:T(4,128)}, u32[]{:S(2)}) copy-start(f32[2,4,1024]{2,1,0:T(4,128)} %param.35) | copy-start | bytes 98308
  668.9 168.2 %copy-start.55 = (f32[2,4,1024]{2,1,0:T(4,128)S(1)}, f32[2,4,1024]{2,1,0:T(4,128)}, u32[]{:S(2)}) copy-start(f32[2,4,1024]{2,1,0:T(4,128)} %param.37) | copy-start | bytes 98308
  668.9 168.2 %copy-start.56 = (f32[2,4,1024]{2,1,0:T(4,128)S(1)}, f32[2,4,1024]{2,1,0:T(4,128)}, u32[]{:S(2)}) copy-start(f32[2,4,1024]{2,1,0:T(4,128)} %param.39) | copy-start | bytes 98308
  (64 other events, 409.3 us)

commit v2 on v1

--- a/solution.py
+++ b/solution.py
@@ -1,3 +1,5 @@
+import functools
+
 import jax
 import jax.numpy as jnp
 from jax import lax
@@ -461,25 +463,32 @@
     dv_ref[0] = dv_acc[...].astype(dv_ref.dtype)
 
 
-def attention_backward(lens, query, key, value, grad, lse):
-    seqs, length, width = query.shape
+def attention_backward(lens, query, key, value, grad, lse, start, grad_start):
+    length, width = query.shape[1:]
+    seqs = lens.shape[0]
     pairs = width // (2 * HEAD)
-    spec = pl.BlockSpec((1, length, 2 * HEAD), lambda s, h, lens: (s, 0, h))
+
+    def block(first):
+        return pl.BlockSpec((1, length, 2 * HEAD), lambda s, h, lens: (s + first, 0, h))
+
     return pl.pallas_call(
         attention_backward_kernel,
         grid_spec=pltpu.PrefetchScalarGridSpec(
             num_scalar_prefetch=1,
             grid=(seqs, pairs),
-            in_specs=[spec] * 4
-            + [pl.BlockSpec((1, 1, 2, length), lambda s, h, lens: (s, h, 0, 0))],
-            out_specs=[spec] * 3,
+            in_specs=[block(start)] * 3
+            + [
+                block(grad_start),
+                pl.BlockSpec((1, 1, 2, length), lambda s, h, lens: (s + start, h, 0, 0)),
+            ],
+            out_specs=[block(0)] * 3,
             scratch_shapes=[
                 pltpu.VMEM((2 * HEAD, length), jnp.bfloat16),
                 pltpu.VMEM((length, 2 * HEAD), jnp.float32),
                 pltpu.VMEM((length, 2 * HEAD), jnp.float32),
             ],
         ),
-        out_shape=[jax.ShapeDtypeStruct(query.shape, jnp.bfloat16)] * 3,
+        out_shape=[jax.ShapeDtypeStruct((seqs, length, width), jnp.bfloat16)] * 3,
         cost_estimate=pl.CostEstimate(
             flops=seqs * width * length * length * 7,
             bytes_accessed=seqs * width * length * 14,
@@ -489,20 +498,450 @@
     )(lens, query, key, value, grad, lse)
 
 
+MID_ROWS = 256
+CHUNK = 1024
+
+
+def centred(values):
+    centre = values - jnp.mean(values, axis=-1, keepdims=True)
+    inverse = lax.rsqrt(jnp.mean(centre * centre, axis=-1, keepdims=True) + 1e-05)
+    return centre * inverse, inverse
+
+
+def norm_backward(grad, gain, normal, inverse):
+    grad = grad * gain
+    mean = jnp.mean(grad, axis=-1, keepdims=True)
+    along = jnp.mean(grad * normal, axis=-1, keepdims=True)
+    return (grad - mean - normal * along) * inverse
+
+
+def dot(a, b):
+    return jnp.dot(a, b, preferred_element_type=jnp.float32)
+
+
+def dot_t(a, b):
+    return lax.dot_general(a, b, NT, preferred_element_type=jnp.float32)
+
+
+def copies_of(pairs, sems):
+    return [pltpu.make_async_copy(a, b, sems.at[i]) for i, (a, b) in enumerate(pairs)]
+
+
+def middle_kernel(
+    table_ref,
+    tokens_ref,
+    cotangent_ref,
+    attended_own,
+    attended_far,
+    out_bias_ref,
+    gain_ref,
+    shift_ref,
+    up_bias_ref,
+    down_bias_ref,
+    out_own,
+    out_near,
+    out_far,
+    up_own,
+    up_near,
+    up_far,
+    down_own,
+    down_near,
+    down_far,
+    block_ref,
+    resid_grad_ref,
+    own_grad_ref,
+    far_grad_ref,
+    out_w,
+    up_w,
+    down_w,
+    residual_ref,
+    normed_ref,
+    normal_ref,
+    acc_ref,
+    grad_acc_ref,
+    sems,
+):
+    step = pl.program_id(0)
+
+    pairs = []
+    start = 0
+    for piece in (out_own, out_near, out_far):
+        rows = piece.shape[0]
+        pairs.append((piece, out_w.at[pl.ds(start, rows), :]))
+        start += rows
+    chunk = 0
+    for up, down in ((up_own, down_own), (up_near, down_near), (up_far, down_far)):
+        for at in range(up.shape[1] // CHUNK):
+            units = pl.ds(at * CHUNK, CHUNK)
+            pairs.append((up.at[:, units], up_w.at[chunk]))
+            pairs.append((down.at[units, :], down_w.at[chunk]))
+            chunk += 1
+    loads = copies_of(pairs, sems)
+
+    @pl.when(step == 0)
+    def _():
+        for load in loads:
+            load.start()
+        for load in loads[:3]:
+            load.wait()
+
+    live = table_ref[2, step]
+    residual = tokens_ref[...].astype(jnp.float32) + (
+        dot(jnp.concatenate((attended_own[...], attended_far[...]), axis=1), out_w[...])
+        + out_bias_ref[...]
+    )
+    residual_ref[...] = residual
+    normal, inverse = centred(residual)
+    normal_ref[...] = normal
+    normed_ref[...] = (normal * gain_ref[...] + shift_ref[...]).astype(jnp.bfloat16)
+    acc_ref[...] = jnp.zeros_like(acc_ref)
+
+    @pl.when(step == 0)
+    def _():
+        for load in loads[3:]:
+            load.wait()
+
+    scale = 0.7978845608028654
+    cube = 0.044715 * scale
+
+    def forward_only(chunk, carry):
+        pre = dot(normed_ref[...], up_w[chunk]) + up_bias_ref[chunk]
+        tanh = jnp.tanh(pre * (scale + cube * (pre * pre)))
+        hidden = (pre * (0.5 + 0.5 * tanh)).astype(jnp.bfloat16)
+        acc_ref[...] += dot(hidden, down_w[chunk])
+        return carry
+
+    def finish():
+        block_ref[...] = (residual_ref[...] + acc_ref[...] + down_bias_ref[...]).astype(
+            block_ref.dtype
+        )
+
+    @pl.when(live > 0)
+    def _():
+        row = lax.broadcasted_iota(jnp.int32, (MID_ROWS, 1), 0)
+        grad_out = jnp.where(row < live, cotangent_ref[...], jnp.zeros((), jnp.bfloat16))
+        grad_acc_ref[...] = jnp.zeros_like(grad_acc_ref)
+
+        def both_ways(chunk, carry):
+            pre = dot(normed_ref[...], up_w[chunk]) + up_bias_ref[chunk]
+            grad_hidden = dot_t(grad_out, down_w[chunk])
+            square = pre * pre
+            tanh = jnp.tanh(pre * (scale + cube * square))
+            gate = 0.5 + 0.5 * tanh
+            hidden = (pre * gate).astype(jnp.bfloat16)
+            slope = gate + (pre * (0.5 - 0.5 * (tanh * tanh))) * (scale + 3.0 * cube * square)
+            grad_pre = (grad_hidden * slope).astype(jnp.bfloat16)
+            acc_ref[...] += dot(hidden, down_w[chunk])
+            grad_acc_ref[...] += dot_t(grad_pre, up_w[chunk])
+            return carry
+
+        lax.fori_loop(0, up_w.shape[0], both_ways, 0, unroll=UNROLL)
+        finish()
+        grad_resid = grad_out.astype(jnp.float32) + norm_backward(
+            grad_acc_ref[...], gain_ref[...], normal_ref[...], inverse
+        )
+        low = grad_resid.astype(jnp.bfloat16)
+        resid_grad_ref[...] = low
+        columns = own_grad_ref.shape[1]
+        own_grad_ref[...] = dot_t(low, out_w[:columns]).astype(jnp.bfloat16)
+        far_grad_ref[...] = dot_t(low, out_w[columns:]).astype(jnp.bfloat16)
+
+    @pl.when(live <= 0)
+    def _():
+        lax.fori_loop(0, up_w.shape[0], forward_only, 0, unroll=UNROLL)
+        finish()
+        resid_grad_ref[...] = jnp.zeros_like(resid_grad_ref)
+        own_grad_ref[...] = jnp.zeros_like(own_grad_ref)
+        far_grad_ref[...] = jnp.zeros_like(far_grad_ref)
+
+
+UNROLL = 2
+
+
+def middle(
+    table, tokens, cotangent, own, far, out_bias, gain, shift, up_bias, down_bias, weights
+):
+    rows, width = far.shape[0], tokens.shape[1]
+    columns = far.shape[1]
+    units = up_bias.shape[0] * up_bias.shape[2]
+    tile = pl.BlockSpec((MID_ROWS, width), lambda i, t: (i, 0))
+    picked = pl.BlockSpec((MID_ROWS, width), lambda i, t: (t[0, i], 0))
+    part = pl.BlockSpec((MID_ROWS, columns), lambda i, t: (i, 0))
+    vector = pl.BlockSpec((1, width), lambda i, t: (0, 0))
+    chunks = units // CHUNK
+    low = jax.ShapeDtypeStruct((rows, width), jnp.bfloat16)
+    thin = jax.ShapeDtypeStruct((rows, columns), jnp.bfloat16)
+    wide = pltpu.VMEM((MID_ROWS, width), jnp.float32)
+    return pl.pallas_call(
+        middle_kernel,
+        grid_spec=pltpu.PrefetchScalarGridSpec(
+            num_scalar_prefetch=1,
+            grid=(rows // MID_ROWS,),
+            in_specs=[picked] * 2
+            + [pl.BlockSpec((MID_ROWS, columns), lambda i, t: (t[1, i], 0)), part]
+            + [vector] * 3
+            + [pl.BlockSpec(up_bias.shape, lambda i, t: (0, 0, 0)), vector]
+            + [pl.BlockSpec(memory_space=pl.ANY)] * 9,
+            out_specs=[tile, tile, part, part],
+            scratch_shapes=[
+                pltpu.VMEM((width, width), jnp.bfloat16),
+                pltpu.VMEM((chunks, width, CHUNK), jnp.bfloat16),
+                pltpu.VMEM((chunks, CHUNK, width), jnp.bfloat16),
+                wide,
+                pltpu.VMEM((MID_ROWS, width), jnp.bfloat16),
+                wide,
+                wide,
+                wide,
+                pltpu.SemaphoreType.DMA((3 + 2 * chunks,)),
+            ],
+        ),
+        out_shape=[low, low, thin, thin],
+        compiler_params=pltpu.CompilerParams(vmem_limit_bytes=56 << 20),
+        cost_estimate=pl.CostEstimate(
+            flops=rows * width * (units * 8 + width * 4),
+            bytes_accessed=rows * width * 12 + units * width * 4,
+            transcendentals=rows * units,
+        ),
+        name="middle",
+    )(
+        table,
+        tokens,
+        cotangent,
+        own,
+        far,
+        out_bias,
+        gain,
+        shift,
+        up_bias,
+        down_bias,
+        *weights,
+    )
+
+
+PROJECT_ROWS = 256
+
+
+def qkv_loads(own, near, far, weight_ref, sems):
+    pairs = []
+    start = 0
+    for piece in (own, near, far):
+        if piece is not None:
+            columns = pl.ds(start, piece.shape[2])
+            pairs.append((piece, weight_ref.at[:, :, columns]))
+            start += piece.shape[2]
+    return copies_of(pairs, sems)
+
+
+def project_kernel(pieces, table_ref, *refs):
+    tokens_ref, gain_ref, shift_ref, down_ref, up_ref = refs[:5]
+    weights = list(refs[5 : 5 + pieces]) + [None] * (3 - pieces)
+    query_ref, key_ref, value_ref, low_ref, weight_ref, sems = refs[5 + pieces :]
+    loads = qkv_loads(*weights, weight_ref, sems)
+    first = pl.program_id(0) == 0
+
+    @pl.when(first)
+    def _():
+        for load in loads:
+            load.start()
+
+    normal, _ = centred(tokens_ref[...].astype(jnp.float32))
+    normed = (normal * gain_ref[...] + shift_ref[...]).astype(jnp.bfloat16)
+    low = dot_t(normed, down_ref[...]).astype(jnp.bfloat16)
+    low_ref[...] = low.astype(jnp.float32).T
+
+    @pl.when(first)
+    def _():
+        for load in loads:
+            load.wait()
+
+    query_ref[...] = (dot(normed, weight_ref[0]) + 8.0 * dot(low, up_ref[0])).astype(jnp.bfloat16)
+    key_ref[...] = dot(normed, weight_ref[1]).astype(jnp.bfloat16)
+    value_ref[...] = (dot(normed, weight_ref[2]) + 8.0 * dot(low, up_ref[1])).astype(jnp.bfloat16)
+
+
+def project(table, tokens, gain, shift, down, up, *weights):
+    rows, width = table.shape[0] * PROJECT_ROWS, tokens.shape[1]
+    columns = up.shape[2]
+    pairs = down.shape[0]
+    out = pl.BlockSpec((PROJECT_ROWS, columns), lambda i, t: (i, 0))
+    vector = pl.BlockSpec((1, width), lambda i, t: (0, 0))
+    return pl.pallas_call(
+        functools.partial(project_kernel, len(weights)),
+        grid_spec=pltpu.PrefetchScalarGridSpec(
+            num_scalar_prefetch=1,
+            grid=(rows // PROJECT_ROWS,),
+            in_specs=[
+                pl.BlockSpec((PROJECT_ROWS, width), lambda i, t: (t[i], 0)),
+                vector,
+                vector,
+                pl.BlockSpec(down.shape, lambda i, t: (0, 0)),
+                pl.BlockSpec(up.shape, lambda i, t: (0, 0, 0)),
+            ]
+            + [pl.BlockSpec(memory_space=pl.ANY)] * len(weights),
+            out_specs=[out] * 3 + [pl.BlockSpec((pairs, PROJECT_ROWS), lambda i, t: (0, i))],
+            scratch_shapes=[
+                pltpu.VMEM((3, width, columns), jnp.bfloat16),
+                pltpu.SemaphoreType.DMA((len(weights),)),
+            ],
+        ),
+        out_shape=[jax.ShapeDtypeStruct((rows, columns), jnp.bfloat16)] * 3
+        + [jax.ShapeDtypeStruct((pairs, rows), jnp.float32)],
+        cost_estimate=pl.CostEstimate(
+            flops=rows * width * columns * 6,
+            bytes_accessed=rows * (width + 3 * columns) * 2 + 6 * width * columns,
+            transcendentals=rows,
+        ),
+        name="project",
+    )(table, tokens, gain, shift, down, up, *weights)
+
+
+def first_backward_kernel(
+    table_ref,
+    tokens_ref,
+    resid_grad_ref,
+    low_ref,
+    query_own,
+    key_own,
+    value_own,
+    query_far,
+    key_far,
+    value_far,
+    gain_ref,
+    shift_ref,
+    down_ref,
+    up_ref,
+    own_ref,
+    near_ref,
+    far_ref,
+    input_ref,
+    down_grad_ref,
+    query_up_ref,
+    value_up_ref,
+    weight_ref,
+    sems,
+):
+    first = pl.program_id(0) == 0
+    loads = qkv_loads(own_ref, near_ref, far_ref, weight_ref, sems)
+
+    @pl.when(first)
+    def _():
+        for load in loads:
+            load.start()
+        down_grad_ref[...] = jnp.zeros_like(down_grad_ref)
+        query_up_ref[...] = jnp.zeros_like(query_up_ref)
+        value_up_ref[...] = jnp.zeros_like(value_up_ref)
+
+    normal, inverse = centred(tokens_ref[...].astype(jnp.float32))
+    normed = (normal * gain_ref[...] + shift_ref[...]).astype(jnp.bfloat16)
+    query = jnp.concatenate((query_own[...], query_far[...]), axis=1)
+    key = jnp.concatenate((key_own[...], key_far[...]), axis=1)
+    value = jnp.concatenate((value_own[...], value_far[...]), axis=1)
+    adapter = 8.0 * (dot_t(query, up_ref[0]) + dot_t(value, up_ref[1]))
+    high = adapter.astype(jnp.bfloat16)
+    rest = (adapter - high.astype(jnp.float32)).astype(jnp.bfloat16)
+    down_grad_ref[...] += dot(high.astype(jnp.float32).T.astype(jnp.bfloat16), normed) + dot(
+        rest.astype(jnp.float32).T.astype(jnp.bfloat16), normed
+    )
+    low = low_ref[...].astype(jnp.bfloat16)
+    query_up_ref[...] += dot(low, query)
+    value_up_ref[...] += dot(low, value)
+
+    @pl.when(first)
+    def _():
+        for load in loads:
+            load.wait()
+
+    grad = (
+        dot_t(query, weight_ref[0])
+        + dot_t(key, weight_ref[1])
+        + dot_t(value, weight_ref[2])
+        + dot(high, down_ref[...])
+        + dot(rest, down_ref[...])
+    )
+    input_ref[...] = (
+        resid_grad_ref[...].astype(jnp.float32)
+        + norm_backward(grad, gain_ref[...], normal, inverse)
+    ).astype(input_ref.dtype)
+
+
+def first_backward(
+    table, tokens, resid_grad, low, own, far, gain, shift, down, up, weights
+):
+    tiles = table.shape[1]
+    rows, width = tiles * PROJECT_ROWS, tokens.shape[1]
+    pairs = down.shape[0]
+    columns = own[0].shape[1]
+    tile = pl.BlockSpec((PROJECT_ROWS, width), lambda i, t: (t[0, i], 0))
+    vector = pl.BlockSpec((1, width), lambda i, t: (0, 0))
+    small = pl.BlockSpec((pairs, width), lambda i, t: (0, 0))
+    sums = jax.ShapeDtypeStruct((pairs, width), jnp.float32)
+    return pl.pallas_call(
+        first_backward_kernel,
+        grid_spec=pltpu.PrefetchScalarGridSpec(
+            num_scalar_prefetch=1,
+            grid=(tiles,),
+            in_specs=[
+                tile,
+                pl.BlockSpec((PROJECT_ROWS, width), lambda i, t: (t[1, i], 0)),
+                pl.BlockSpec((pairs, PROJECT_ROWS), lambda i, t: (0, t[2, i])),
+            ]
+            + [pl.BlockSpec((PROJECT_ROWS, columns), lambda i, t: (t[3, i], 0))] * 3
+            + [pl.BlockSpec((PROJECT_ROWS, columns), lambda i, t: (i, 0))] * 3
+            + [vector, vector, small, pl.BlockSpec(up.shape, lambda i, t: (0, 0, 0))]
+            + [pl.BlockSpec(memory_space=pl.ANY)] * 3,
+            out_specs=[pl.BlockSpec((PROJECT_ROWS, width), lambda i, t: (i, 0))] + [small] * 3,
+            scratch_shapes=[
+                pltpu.VMEM((3, width, width), jnp.bfloat16),
+                pltpu.SemaphoreType.DMA((3,)),
+            ],
+        ),
+        out_shape=[jax.ShapeDtypeStruct((rows, width), jnp.bfloat16)] + [sums] * 3,
+        cost_estimate=pl.CostEstimate(
+            flops=rows * width * width * 7,
+            bytes_accessed=rows * width * 12 + 6 * width * width,
+            transcendentals=rows,
+        ),
+        name="first_backward",
+    )(table, tokens, resid_grad, low, *own, *far, gain, shift, down, up, *weights)
+
+
 def swap(value):
     return lax.ppermute(value, "mp", [(0, 1), (1, 0)])
 
 
-def partner_shard(shard, axis):
+def after(value, *earlier):
+    return lax.optimization_barrier((value, *earlier))[0]
+
+
+def core_swap(value):
+    return lax.ppermute(value, "dp", [(i, i ^ 1) for i in range(lax.axis_size("dp"))])
+
+
+def core_half(shard, axis):
     size = shard.shape[axis] // 2
     core = lax.rem(lax.axis_index("dp"), 2)
+    return lax.dynamic_slice_in_dim(shard, core * size, size, axis)
+
+
+def core_order(value, axis):
+    size = value.shape[axis] // 2
+    core = lax.rem(lax.axis_index("dp"), 2)
+    low = lax.slice_in_dim(value, 0, size, axis=axis)
+    high = lax.slice_in_dim(value, size, 2 * size, axis=axis)
+    return jnp.where(
+        core == 0, value, jnp.concatenate((high, low), axis=axis)
+    )
+
+
+def sum_all(value):
     count = lax.axis_size("dp")
-    half = lax.dynamic_slice_in_dim(shard, core * size, size, axis)
-    mine = swap(half)
-    other = lax.ppermute(mine, "dp", [(i, i ^ 1) for i in range(count)])
-    low = jnp.where(core == 0, mine, other)
-    high = jnp.where(core == 0, other, mine)
-    return jnp.concatenate((shard, low, high), axis=axis)
+    if count & (count - 1):
+        return lax.psum(value, ("dp", "mp"))
+    bit = 1
+    while bit < count:
+        value = value + lax.ppermute(value, "dp", [(i, i ^ bit) for i in range(count)])
+        bit *= 2
+    return value + swap(value)
 
 
 def per_device_pair(
@@ -528,182 +967,226 @@
     up_second_moment,
 ):
     f32, bf16 = jnp.float32, jnp.bfloat16
-    length, width = tokens.shape[1:]
+    seqs, length, width = tokens.shape
     rank = adapter_down_factor.shape[2]
     me = lax.axis_index("mp")
-    half_width = query_key_value_weight.shape[2]
+    columns = query_key_value_weight.shape[2]
     whole, half = 2, length // 2
     split = 2 * whole
-
-    def own(array, half_at):
-        entire = lax.dynamic_slice_in_dim(array, whole * me, whole, 0)
-        part = lax.dynamic_slice_in_dim(array[split], half_at * half, half, 0)
-        return jnp.concatenate((entire.reshape(whole * length, width), part), axis=0)
-
-    qkv_full = partner_shard(query_key_value_weight, 2)
-    out_full = partner_shard(attention_output_weight, 0)
-    up_full = partner_shard(feedforward_up_weight, 1)
-    up_bias = jnp.concatenate((feedforward_up_bias, swap(feedforward_up_bias)))
-    down_full = partner_shard(feedforward_down_weight, 0)
-
-    def own_first(array):
-        mine = lax.dynamic_slice_in_dim(array, me * half_width, half_width, 2)
-        theirs = lax.dynamic_slice_in_dim(array, (1 - me) * half_width, half_width, 2)
-        return mine, jnp.concatenate((mine, theirs), axis=2)
-
-    down_low = adapter_down_factor.astype(bf16)
-    down_pair = jnp.concatenate((down_low[0], down_low[1]), axis=1)
-    up_mine, up_ordered = own_first(adapter_up_factor.astype(bf16))
-
-    def dot(a, b):
-        return jnp.dot(a, b, preferred_element_type=f32)
-
-    def dot_t(a, b):
-        return lax.dot_general(a, b, NT, preferred_element_type=f32)
-
-    def project(rows, weight, up):
-        normed = layer_norm(rows.astype(f32), first_norm_gain, first_norm_bias).astype(bf16)
-        low = dot(normed, down_pair).astype(bf16)
-        query = (dot(normed, weight[0]) + 8.0 * dot(low[:, :rank], up[0])).astype(bf16)
-        key = dot(normed, weight[1]).astype(bf16)
-        value = (dot(normed, weight[2]) + 8.0 * dot(low[:, rank:], up[1])).astype(bf16)
-        return normed, low, query, key, value
+    tiles, half_tiles = length // MID_ROWS, half // MID_ROWS
+
+    def row(vector):
+        return vector.reshape(1, -1)
+
+    qkv_near = swap(core_half(query_key_value_weight, 2))
+    qkv_far = core_swap(qkv_near)
+    out_near = swap(after(core_half(attention_output_weight, 0), qkv_near))
+    out_far = core_swap(out_near)
+    up_near = swap(after(core_half(feedforward_up_weight, 1), out_near))
+    up_far = core_swap(up_near)
+    down_near = swap(after(core_half(feedforward_down_weight, 0), up_near))
+    down_far = core_swap(down_near)
+    qkv = (query_key_value_weight, qkv_near, qkv_far)
+    up_bias = jnp.concatenate(
+        (feedforward_up_bias, core_order(swap(feedforward_up_bias), 0))
+    ).reshape(-1, 1, CHUNK)
+
+    down_low = adapter_down_factor.astype(bf16).transpose(0, 2, 1).reshape(2 * rank, width)
+    up_low = adapter_up_factor.astype(bf16)
+    blank = jnp.zeros_like(up_low[0])
+    up_low = jnp.stack(
+        (jnp.concatenate((up_low[0], blank)), jnp.concatenate((blank, up_low[1])))
+    )
+    up_own = lax.dynamic_slice_in_dim(up_low, me * columns, columns, 2)
+    up_other = core_order(
+        lax.dynamic_slice_in_dim(up_low, (1 - me) * columns, columns, 2), 2
+    )
+    up_both = jnp.concatenate((up_own, up_other), axis=2)
 
     own_lens = lax.dynamic_slice_in_dim(lengths, whole * me, whole, 0)
     split_lens = lengths[split:]
-    own_tokens = own(tokens, me)
-    normed_s, low_s, query_s, key_s, value_s = project(
-        tokens[split], query_key_value_weight, up_mine
-    )
-    heads_s = [piece[None] for piece in (query_s, key_s, value_s)]
-    attended_s, lse_s = attention_forward(split_lens, *heads_s)
-    attended_s = attended_s[0]
-
-    def mine_rows(array):
-        return lax.dynamic_slice_in_dim(array, me * half, half, 0)
-
-    def theirs_rows(array):
-        return lax.dynamic_slice_in_dim(array, (1 - me) * half, half, 0)
-
-    attended_got = swap(theirs_rows(attended_s))
-    normed_w, low_w, query_w, key_w, value_w = project(
-        own_tokens[: whole * length], qkv_full, up_ordered
-    )
-    heads_w = [piece.reshape(whole, length, width) for piece in (query_w, key_w, value_w)]
-    attended_w, lse_w = attention_forward(own_lens, *heads_w)
-    attended = jnp.concatenate(
+    three_lens = jnp.concatenate((own_lens, split_lens))
+    flat_tokens = tokens.reshape(-1, width)
+    flat_cotangent = cotangent.reshape(-1, width)
+    step = jnp.arange(whole * tiles, dtype=jnp.int32)
+    extra = jnp.arange(half_tiles, dtype=jnp.int32) + me * half_tiles
+    whole_table = step + whole * me * tiles
+    token_table = jnp.concatenate((whole_table, split * tiles + extra))
+    own_table = jnp.concatenate((step, whole * tiles + extra))
+    live_table = jnp.concatenate(
         (
-            attended_w.reshape(whole * length, width),
-            jnp.concatenate((mine_rows(attended_s), attended_got), axis=1),
-        ),
-        axis=0,
-    )
-    tokens_f32 = own_tokens.astype(f32)
-
-    def norm_two(values):
-        return layer_norm(values, second_norm_gain, second_norm_bias)
-
-    def norm_one(values):
-        return layer_norm(values, first_norm_gain, first_norm_bias)
-
-    residual = tokens_f32 + (dot(attended, out_full) + attention_output_bias)
-    normed_two = norm_two(residual).astype(bf16)
-    hidden_pre = dot(normed_two, up_full) + up_bias
-    hidden = gelu_tanh(hidden_pre).astype(bf16)
-    block_own = (residual + dot(hidden, down_full) + feedforward_down_bias).astype(bf16)
-    block_got = swap(block_own)
-
-    def both(mine, got):
-        first = jnp.where(me == 0, mine, got)
-        second = jnp.where(me == 0, got, mine)
-        parts = (
-            first[: whole * length],
-            second[: whole * length],
-            first[whole * length :],
-            second[whole * length :],
+            own_lens[step // tiles] - (step % tiles) * MID_ROWS,
+            split_lens[0] - extra * MID_ROWS,
         )
-        return jnp.concatenate(parts, axis=0).reshape(tokens.shape)
-
-    block_out = both(block_own, block_got)
-    at = jnp.arange(length)
-    live = jnp.concatenate(
+    )
+    three_table = jnp.concatenate(
+        (whole_table, split * tiles + jnp.arange(tiles, dtype=jnp.int32))
+    )
+    gain_one, shift_one = row(first_norm_gain), row(first_norm_bias)
+
+    def sequences(pieces):
+        return [piece.reshape(-1, length, columns) for piece in pieces]
+
+    *own_heads, low = project(
+        three_table,
+        flat_tokens,
+        gain_one,
+        shift_one,
+        down_low,
+        up_own,
+        query_key_value_weight,
+    )
+    own_heads = sequences(own_heads)
+    attended_own, lse_own = attention_forward(three_lens, *own_heads)
+    sent = lax.dynamic_slice_in_dim(attended_own[whole], (1 - me) * half, half, 0)
+    attended_got = swap(core_order(sent, 1))
+    *far_heads, _ = project(
+        whole_table,
+        flat_tokens,
+        gain_one,
+        shift_one,
+        down_low,
+        up_other,
+        qkv_near,
+        after(qkv_far, attended_own),
+    )
+    far_heads = sequences(far_heads)
+    attended_far, lse_far = attention_forward(own_lens, *far_heads)
+    block_own, resid_grad, grad_own, grad_far = middle(
+        jnp.stack((token_table, own_table, live_table)),
+        flat_tokens,
+        flat_cotangent,
+        attended_own.reshape(-1, columns),
+        jnp.concatenate((attended_far.reshape(-1, columns), attended_got), axis=0),
+        row(attention_output_bias),
+        row(second_norm_gain),
+        row(second_norm_bias),
+        up_bias,
+        row(feedforward_down_bias),
         (
-            (at[None, :] < own_lens[:, None]).reshape(-1, 1),
-            (mine_rows(at) < split_lens[0]).reshape(-1, 1),
-        ),
-        axis=0,
-    )
-    grad_out = jnp.where(live, own(cotangent, me), jnp.zeros((), bf16))
-    grad_hidden = dot_t(grad_out, down_full)
-    _, gelu_back = jax.vjp(gelu_tanh, hidden_pre)
-    grad_pre = gelu_back(grad_hidden)[0].astype(bf16)
-    grad_norm2 = dot_t(grad_pre, up_full)
-    _, norm2_back = jax.vjp(norm_two, residual)
-    grad_resid = grad_out.astype(f32) + norm2_back(grad_norm2)[0]
-    grad_attended = dot_t(grad_resid.astype(bf16), out_full).astype(bf16)
-    grad_got = swap(grad_attended[whole * length :, half_width:])
-    grad_kept = grad_attended[whole * length :, :half_width]
-    grad_s = jnp.concatenate(
+            attention_output_weight,
+            out_near,
+            out_far,
+            feedforward_up_weight,
+            up_near,
+            up_far,
+            feedforward_down_weight,
+            down_near,
+            down_far,
+        ),
+    )
+    grad_got = swap(core_order(grad_far[whole * length :], 1))
+    block_got = swap(after(block_own, grad_got))
+    grad_kept = grad_own[whole * length :]
+    grad_split = jnp.concatenate(
+        (jnp.where(me == 0, grad_kept, grad_got), jnp.where(me == 0, grad_got, grad_kept))
+    )
+    grad_own = grad_own[: whole * length].reshape(whole, length, columns)
+    grad_far = grad_far[: whole * length].reshape(whole, length, columns)
+
+    def flat(pieces):
+        return [piece.reshape(-1, columns) for piece in pieces]
+
+    def back_whole(index):
+        lens = own_lens[index : index + 1]
+        own = attention_backward(lens, *own_heads, grad_own, lse_own, index, index)
+        far = attention_backward(lens, *far_heads, grad_far, lse_far, index, index)
+        return flat(own), flat(far)
+
+    span = jnp.arange(tiles, dtype=jnp.int32)
+
+    def back_first(own, far, table):
+        return first_backward(
+            table,
+            flat_tokens,
+            resid_grad,
+            low,
+            own,
+            far,
+            gain_one,
+            shift_one,
+            down_low,
+            up_both,
+            qkv,
+        )
+
+    def whole_rows(index):
+        at = index * tiles + span
+        return jnp.stack((whole * me * tiles + at, at, at, span))
+
+    back_zero = back_whole(0)
+    split_own = attention_backward(
+        split_lens, *own_heads, grad_split[None], lse_own, whole, 0
+    )
+    split_sent = jnp.stack(
+        [lax.dynamic_slice_in_dim(p[0], (1 - me) * half, half, 0) for p in split_own]
+    )
+    split_got = swap(
+        core_order(split_sent, 2)
+    )
+    first_zero = back_first(*back_zero, whole_rows(0))
+    send_zero = swap(first_zero[0])
+    back_one = back_whole(1)
+    first_split = back_first(
+        flat(split_own),
+        [split_got[i] for i in range(3)],
+        jnp.stack(
+            (
+                split * tiles + extra,
+                whole * tiles + extra - me * half_tiles,
+                whole * tiles + extra,
+                extra,
+            )
+        ),
+    )
+    send_split = swap(first_split[0])
+    first_one = back_first(*back_one, whole_rows(1))
+    send_one = swap(first_one[0])
+
+    down_sum, query_sum, value_sum = (
+        first_zero[i] + first_split[i] + first_one[i] for i in range(1, 4)
+    )
+    up_sum = 8.0 * jnp.concatenate((query_sum[:rank], value_sum[rank:]))
+    up_mine = up_sum[:, :columns]
+    up_theirs = core_order(up_sum[:, columns:], 1)
+    up_sum = jnp.concatenate(
+        (jnp.where(me == 0, up_mine, up_theirs), jnp.where(me == 0, up_theirs, up_mine)), axis=1
+    )
+    live_row = jnp.full((8, width), jnp.sum(lengths).astype(f32))
+    total = sum_all(jnp.concatenate((down_sum, up_sum, live_row)))
+    active = total[-1, 0] / 2
+    grad_down = total[: 2 * rank].reshape(2, rank, width).transpose(0, 2, 1) / active
+    grad_up = total[2 * rank : 4 * rank].reshape(2, rank, width) / active
+
+    def place(pieces):
+        out = jnp.zeros((seqs * length, width), bf16)
+        for piece, start in pieces:
+            out = lax.dynamic_update_slice_in_dim(out, piece, start, 0)
+        return out.reshape(tokens.shape)
+
+    mine, theirs = whole * length * me, whole * length * (1 - me)
+    block_out = place(
         (
-            jnp.where(me == 0, grad_kept, grad_got),
-            jnp.where(me == 0, grad_got, grad_kept),
-        ),
-        axis=0,
-    )
-    grads_s = attention_backward(split_lens, *heads_s, grad_s[None], lse_s)
-    grads_w = attention_backward(
-        own_lens,
-        *heads_w,
-        grad_attended[: whole * length].reshape(whole, length, width),
-        lse_w,
-    )
-    pack_s = jnp.stack([piece[0] for piece in grads_s])
-    sent = swap(lax.dynamic_slice_in_dim(pack_s, (1 - me) * half, half, 1))
-    kept = lax.dynamic_slice_in_dim(pack_s, me * half, half, 1)
-    tail = jnp.concatenate((kept, sent), axis=2)
-    grad_query, grad_key, grad_value = (
-        jnp.concatenate((grads_w[i].reshape(whole * length, width), tail[i]), axis=0)
-        for i in range(3)
-    )
-    adapter_gradient = 8.0 * jnp.concatenate(
-        (dot_t(grad_query, up_ordered[0]), dot_t(grad_value, up_ordered[1])), axis=1
-    )
-    grad_norm1 = (
-        dot_t(grad_query, qkv_full[0])
-        + dot_t(grad_key, qkv_full[1])
-        + dot_t(grad_value, qkv_full[2])
-        + jnp.einsum(
-            "gy,wy->gw", adapter_gradient, down_pair.astype(f32), precision=lax.Precision.HIGHEST
+            (block_own[: whole * length], mine),
+            (block_own[whole * length :], split * length + half * me),
+            (block_got[: whole * length], theirs),
+            (block_got[whole * length :], split * length + half * (1 - me)),
         )
     )
-    _, norm1_back = jax.vjp(norm_one, tokens_f32)
-    input_own = (grad_resid + norm1_back(grad_norm1)[0]).astype(bf16)
-    input_grad = both(input_own, swap(input_own))
-
-    normed = jnp.concatenate((normed_w, mine_rows(normed_s)), axis=0)
-    low = jnp.concatenate((low_w, mine_rows(low_s)), axis=0)
-    grad_down_both = jnp.einsum(
-        "fi,fg->ig", normed.astype(f32), adapter_gradient, precision=lax.Precision.HIGHEST
-    )
-    grad_down = jnp.stack((grad_down_both[:, :rank], grad_down_both[:, rank:]))
-    grad_up = 8.0 * jnp.stack(
+    input_grad = place(
         (
-            jnp.einsum("zm,zj->mj", low[:, :rank], grad_query, preferred_element_type=f32),
-            jnp.einsum("zm,zj->mj", low[:, rank:], grad_value, preferred_element_type=f32),
+            (first_zero[0], mine),
+            (first_split[0], split * length + half * me),
+            (first_one[0], mine + length),
+            (send_zero, theirs),
+            (send_split, split * length + half * (1 - me)),
+            (send_one, theirs + length),
         )
     )
-    first = jnp.where(me == 0, grad_up[:, :, :half_width], grad_up[:, :, half_width:])
-    second = jnp.where(me == 0, grad_up[:, :, half_width:], grad_up[:, :, :half_width])
-    grad_up = jnp.concatenate((first, second), axis=2)
-    live_local = jnp.sum(lengths).astype(f32)
-    down_sum, up_sum, live_sum = lax.psum((grad_down, grad_up, live_local), ("dp", "mp"))
-    active = live_sum / 2
     new_down = adam_decay_update(
-        adapter_down_factor, down_sum / active, down_first_moment, down_second_moment
-    )
-    new_up = adam_decay_update(
-        adapter_up_factor, up_sum / active, up_first_moment, up_second_moment
-    )
+        adapter_down_factor, grad_down, down_first_moment, down_second_moment
+    )
+    new_up = adam_decay_update(adapter_up_factor, grad_up, up_first_moment, up_second_moment)
     return (
         block_out,
         input_grad,

time: 928 us -> 758 us (0.82)
  matrix products: 303 us -> 0 us
  Pallas kernels: 126 us -> 392 us
  waiting for transfers between devices: 35 us -> 200 us
  blocking collectives: 161 us -> 0 us
  other arithmetic: 113 us -> 19.1 us
  local copies, waits for them, and re-layouts: 105 us -> 59.7 us
  starting transfers between devices: 65.9 us -> 77.5 us
    dot_general x27 -> x0, matrix products: 303 us -> none  [the longest x8 153 us: dot_t(): return lax.dot_general(a, b, NT, preferred_element_type=f32)]
    pallas_call x0 -> x6, Pallas kernels: none -> 207 us  [the longest x1 106 us: middle(): pl.pallas_call(middle_kernel, grid_spec=pltpu.PrefetchScalarGridSpec(num_...]
    psum x1 -> x0, blocking collectives: 161 us -> none  [per_device_pair(): lax.psum((grad_down, grad_up, live_local), ('dp', 'mp'))]
    ppermute x10 -> x13, waiting for transfers between devices: 34.9 us -> 190 us  [swap(): return lax.ppermute(value, 'mp', [(0, 1), (1, 0)])]
    pallas_call x2 -> x5, Pallas kernels: 49.4 us -> 99.2 us  [attention_backward(): pl.pallas_call(attention_backward_kernel, grid_spec=pltpu.PrefetchScalarG...]
    reduce_sum x9 -> x1, other arithmetic: 36.1 us -> 0.63 us  [per_device_pair(): live_row = jnp.full((8, width), jnp.sum(lengths).astype(f32))]
    concatenate x2 -> x1, local copies, waits for them, and re-layouts: 28.8 us -> 0.61 us  [per_device_pair(): total = sum_all(jnp.concatenate((down_sum, up_sum, live_row)))]
    select_n x7, other arithmetic: 27.4 us -> 3.34 us  [the longest x5 3.32 us: core_order(): return jnp.where(core == 0, value, jnp.concatenate((high, low), axis=axis))]
  transfers between devices with their start and end apart: 14 -> 21, of which waited for: 2 -> 6; matrix products, arithmetic and copies ran while one was open for 35% -> 8% of each run, Pallas kernels for 12% -> 38%
where the time goes in v2:
time: 758 us; the launch traced here: 751 us
  Pallas kernels  392 us (52%)
  waiting for transfers between devices  200 us (26%)
  starting transfers between devices  77.5 us (10%)
  local copies, waits for them, and re-layouts  59.7 us (8%)
  other arithmetic  19.1 us (3%)
    ppermute x13, waiting for transfers between devices, swap(): return lax.ppermute(value, 'mp', [(0, 1), (1, 0)])  190 us
    pallas_call x1, Pallas kernels, middle(): pl.pallas_call(middle_kernel, grid_spec=pltpu.PrefetchScalarGridSpec(num_...  106 us
    pallas_call x5, Pallas kernels, attention_backward(): pl.pallas_call(attention_backward_kernel, grid_spec=pltpu.PrefetchScalarG...  99.2 us
    pallas_call x2, Pallas kernels, attention_forward(): pl.pallas_call(attention_forward_kernel, grid_spec=pltpu.PrefetchScalarGr...  85.5 us
    ppermute x13, starting transfers between devices, swap(): return lax.ppermute(value, 'mp', [(0, 1), (1, 0)])  65.3 us
    pallas_call x3, Pallas kernels, first_backward(): pl.pallas_call(first_backward_kernel, grid_spec=pltpu.PrefetchScalarGridS...  55.2 us
    pallas_call x2, Pallas kernels, project(): pl.pallas_call(functools.partial(project_kernel, len(weights)), grid_spec...  46.3 us
    dynamic_update_slice x10, local copies, waits for them, and re-layouts, place(): out = lax.dynamic_update_slice_in_dim(out, piece, start, 0)  24.1 us
  transfers between devices with their start and end apart: 21, of which 6 were waited for; matrix products, arithmetic and copies ran while one was open for 8% of the time, Pallas kernels for 38%

profile of v2, /device:TPU:31, one launch (start us, length us, event | category | flops | bytes accessed | tf_op | source)
XLA Modules:
  0.0 750.9 jit_solution(16338932128590568118)
XLA Ops:
  4.4 33.1 %collective-permute-done.refs_5_.near_ref = bf16[3,1024,256]{2,1,0:T(8,128)(2,1)S(1)} collective-permute-done((bf16[3,1024,256]{2,1,0:T(8,128)(2,1)S(1)}, bf16[3,1024,256]{2,1,0:T(8,128)(2,1)S(1)}, u32[]{:S(2)}, u32[]{:S(2)}) %collective-permute-start) | collective-permute-done | bytes 1572896 | tf_op jit(solution)/shard_map/ppermute | solution.py:909
  44.8 4.9 collective-permute-done.4.out_near
  49.9 27.0 %project.2 = (bf16[3072,512]{1,0:T(8,128)(2,1)}, bf16[3072,512]{1,0:T(8,128)(2,1)}, bf16[3072,512]{1,0:T(8,128)(2,1)}, f32[8,3072]{1,0:T(8,128)}) custom-call(s32[12]{0:T(128)} %pad_add_fusion.5.table_ref, bf16[5120,1024]{1,0:T(8,128)(2,1)} %bitcast.76, f32[1,1024]{1,0:T(1,128)} %bitcast.105, f32[1,1024]{1,0:T(1,128)} %bitcast.110, ...), custom_call_target="tpu_custom_call" | custom-call | flops 9663676416 | bytes 18874368 | tf_op jit(solution)/shard_map/project/pallas_call | solution.py:768
  77.0 50.1 %attention_forward.2 = (bf16[3,1024,512]{2,1,0:T(8,128)(2,1)}, f32[3,4,2,1024]{3,2,1,0:T(2,128)}) custom-call(s32[3]{0:T(128)} %pad_add_fusion.4.lens_ref, bf16[3,1024,512]{2,1,0:T(8,128)(2,1)} %bitcast.122, bf16[3,1024,512]{2,1,0:T(8,128)(2,1)} %bitcast.126, bf16[3,1024,512]{2,1,0:T(8,128)(2,1)} %bitcast.130), custom_call_target="tpu_custom_call" | custom-call | flops 4831838208 | bytes 12582912 | tf_op jit(solution)/shard_map/attention_forward/pallas_call | solution.py:380
  129.6 3.7 collective-permute-start.2
  139.0 4.0 collective-permute-start.1
  144.2 42.6 %collective-permute-done.8.down_near = bf16[1024,1024]{1,0:T(8,128)(2,1)} collective-permute-done((bf16[1024,1024]{1,0:T(8,128)(2,1)}, bf16[1024,1024]{1,0:T(8,128)(2,1)}, u32[]{:S(2)}, u32[]{:S(2)}) %collective-permute-start.8) | collective-permute-done | bytes 2097184 | tf_op jit(solution)/shard_map/ppermute | solution.py:909
  186.9 4.7 collective-permute-start.9
  195.9 19.3 %project.3 = (bf16[2048,512]{1,0:T(8,128)(2,1)}, bf16[2048,512]{1,0:T(8,128)(2,1)}, bf16[2048,512]{1,0:T(8,128)(2,1)}, f32[8,2048]{1,0:T(8,128)}) custom-call(s32[8]{0:T(128)} %copy-done.26, bf16[5120,1024]{1,0:T(8,128)(2,1)} %bitcast.77, f32[1,1024]{1,0:T(1,128)} %bitcast.106, f32[1,1024]{1,0:T(1,128)} %bitcast.111, ...), custom_call_target="tpu_custom_call" | custom-call | flops 6442450944 | bytes 13631488 | tf_op jit(solution)/shard_map/project/pallas_call | solution.py:768
  215.2 35.4 %attention_forward.3 = (bf16[2,1024,512]{2,1,0:T(8,128)(2,1)}, f32[2,4,2,1024]{3,2,1,0:T(2,128)}) custom-call(s32[2]{0:T(128)} %copy-done, bf16[2,1024,512]{2,1,0:T(8,128)(2,1)} %bitcast.134, bf16[2,1024,512]{2,1,0:T(8,128)(2,1)} %bitcast.137, bf16[2,1024,512]{2,1,0:T(8,128)(2,1)} %bitcast.140), custom_call_target="tpu_custom_call" | custom-call | flops 3221225472 | bytes 8388608 | tf_op jit(solution)/shard_map/attention_forward/pallas_call | solution.py:380
  250.5 3.4 pad_maximum_fusion.attended_far
  253.9 105.9 %middle.1 = (bf16[2560,1024]{1,0:T(8,128)(2,1)}, bf16[2560,1024]{1,0:T(8,128)(2,1)}, bf16[2560,512]{1,0:T(8,128)(2,1)}, bf16[2560,512]{1,0:T(8,128)(2,1)}) custom-call(s32[3,10]{1,0:T(4,128)} %pad_add_fusion.2.table_ref, bf16[5120,1024]{1,0:T(8,128)(2,1)} %bitcast.78, bf16[5120,1024]{1,0:T(8,128)(2,1)} %bitcast.117, bf16[3072,512]{1,0:T(8,128)(2,1)} %bitcast.104, ...), custom_call_target="tpu_custom_call" | custom-call | flops 96636764160 | bytes 48234496 | tf_op jit(solution)/shard_map/middle/pallas_call | solution.py:675
  359.8 3.2 slice.131
  367.5 25.4 %collective-permute-start.10 = (bf16[512,512]{1,0:T(8,128)(2,1)}, bf16[512,512]{1,0:T(8,128)(2,1)S(1)}, u32[]{:S(2)}, u32[]{:S(2)}) collective-permute-start(bf16[512,512]{1,0:T(8,128)(2,1)} %maximum_select_fusion.2), channel_id=1, source_target_pairs={{0,1},{1,0},{2,3},{3,2},{4,5},{5,4},{6,7},{7,6},{8,9},{9,8},{10,11... | collective-permute-start | bytes 1572872 | tf_op jit(solution)/shard_map/ppermute | solution.py:909
  392.9 13.7 %attention_backward.6 = (bf16[1,1024,512]{2,1,0:T(8,128)(2,1)}, bf16[1,1024,512]{2,1,0:T(8,128)(2,1)}, bf16[1,1024,512]{2,1,0:T(8,128)(2,1)}) custom-call(s32[1]{0:T(128)} %get-tuple-element.134.lens_ref, bf16[2,1024,512]{2,1,0:T(8,128)(2,1)} %bitcast.135, bf16[2,1024,512]{2,1,0:T(8,128)(2,1)} %bitcast.138, bf16[2,1024,512]{2,1,0:T(8,128)(2,1)} %bitcast.141, ...), custom_call_target="tpu_custom_call" | custom-call | flops 3758096384 | bytes 7340032 | tf_op jit(solution)/shard_map/attention_backward/pallas_call | solution.py:474
  406.6 13.5 %attention_backward.5 = (bf16[1,1024,512]{2,1,0:T(8,128)(2,1)}, bf16[1,1024,512]{2,1,0:T(8,128)(2,1)}, bf16[1,1024,512]{2,1,0:T(8,128)(2,1)}) custom-call(s32[1]{0:T(128)} %get-tuple-element.134.lens_ref, bf16[3,1024,512]{2,1,0:T(8,128)(2,1)} %bitcast.123, bf16[3,1024,512]{2,1,0:T(8,128)(2,1)} %bitcast.127, bf16[3,1024,512]{2,1,0:T(8,128)(2,1)} %bitcast.131, ...), custom_call_target="tpu_custom_call" | custom-call | flops 3758096384 | bytes 7340032 | tf_op jit(solution)/shard_map/attention_backward/pallas_call | solution.py:474
  420.1 21.2 %first_backward.3 = (bf16[1024,1024]{1,0:T(8,128)(2,1)}, f32[8,1024]{1,0:T(8,128)}, f32[8,1024]{1,0:T(8,128)}, f32[8,1024]{1,0:T(8,128)}) custom-call(s32[4,4]{1,0:T(4,128)} %get-tuple-element.136.table_ref, bf16[5120,1024]{1,0:T(8,128)(2,1)} %bitcast.79, bf16[2560,1024]{1,0:T(8,128)(2,1)} %get-tuple-element.70.resid_grad_ref, ...), custom_call_target="tpu_custom_call" | custom-call | flops 7516192768 | bytes 18874368 | tf_op jit(solution)/shard_map/first_backward/pallas_call | solution.py:878
  441.3 31.3 %collective-permute-start.13 = (bf16[1024,1024]{1,0:T(8,128)(2,1)}, bf16[1024,1024]{1,0:T(8,128)(2,1)}, u32[]{:S(2)}, u32[]{:S(2)}) collective-permute-start(bf16[1024,1024]{1,0:T(8,128)(2,1)} %get-tuple-element.81), channel_id=1, source_target_pairs={{0,1},{1,0},{2,3},{3,2},{4,5},{5,4},{6,7},{7,6},{8,9},{9,8},{10,11... | collective-permute-start | bytes 6291464 | tf_op jit(solution)/shard_map/ppermute | solution.py:909
  472.6 29.1 %attention_backward.9 = (bf16[1,1024,512]{2,1,0:T(8,128)(2,1)}, bf16[1,1024,512]{2,1,0:T(8,128)(2,1)}, bf16[1,1024,512]{2,1,0:T(8,128)(2,1)}) custom-call(s32[1]{0:T(128)} %get-tuple-element.133.lens_ref, bf16[2,1024,512]{2,1,0:T(8,128)(2,1)} %bitcast.136, bf16[2,1024,512]{2,1,0:T(8,128)(2,1)} %bitcast.139, bf16[2,1024,512]{2,1,0:T(8,128)(2,1)} %bitcast.142, ...), custom_call_target="tpu_custom_call" | custom-call | flops 3758096384 | bytes 7340032 | tf_op jit(solution)/shard_map/attention_backward/pallas_call | solution.py:474
  502.9 13.6 %attention_backward.7 = (bf16[1,1024,512]{2,1,0:T(8,128)(2,1)}, bf16[1,1024,512]{2,1,0:T(8,128)(2,1)}, bf16[1,1024,512]{2,1,0:T(8,128)(2,1)}) custom-call(s32[1]{0:T(128)} %slice.112.lens_ref, bf16[3,1024,512]{2,1,0:T(8,128)(2,1)} %bitcast.124, bf16[3,1024,512]{2,1,0:T(8,128)(2,1)} %bitcast.128, bf16[3,1024,512]{2,1,0:T(8,128)(2,1)} %bitcast.132, ...), custom_call_target="tpu_custom_call" | custom-call | flops 3758096384 | bytes 7340032 | tf_op jit(solution)/shard_map/attention_backward/pallas_call | solution.py:474
  520.5 29.3 %attention_backward.8 = (bf16[1,1024,512]{2,1,0:T(8,128)(2,1)}, bf16[1,1024,512]{2,1,0:T(8,128)(2,1)}, bf16[1,1024,512]{2,1,0:T(8,128)(2,1)}) custom-call(s32[1]{0:T(128)} %get-tuple-element.133.lens_ref, bf16[3,1024,512]{2,1,0:T(8,128)(2,1)} %bitcast.125, bf16[3,1024,512]{2,1,0:T(8,128)(2,1)} %bitcast.129, bf16[3,1024,512]{2,1,0:T(8,128)(2,1)} %bitcast.133, ...), custom_call_target="tpu_custom_call" | custom-call | flops 3758096384 | bytes 7340032 | tf_op jit(solution)/shard_map/attention_backward/pallas_call | solution.py:474
  551.2 20.8 %first_backward.5 = (bf16[1024,1024]{1,0:T(8,128)(2,1)}, f32[8,1024]{1,0:T(8,128)}, f32[8,1024]{1,0:T(8,128)}, f32[8,1024]{1,0:T(8,128)}) custom-call(s32[4,4]{1,0:T(4,128)} %get-tuple-element.135.table_ref, bf16[5120,1024]{1,0:T(8,128)(2,1)} %bitcast.80, bf16[2560,1024]{1,0:T(8,128)(2,1)} %get-tuple-element.70.resid_grad_ref, ...), custom_call_target="tpu_custom_call" | custom-call | flops 7516192768 | bytes 18874368 | tf_op jit(solution)/shard_map/first_backward/pallas_call | solution.py:878
  572.1 5.4 broadcast.180.clone
  581.4 13.2 %first_backward.4 = (bf16[512,1024]{1,0:T(8,128)(2,1)}, f32[8,1024]{1,0:T(8,128)}, f32[8,1024]{1,0:T(8,128)}, f32[8,1024]{1,0:T(8,128)}) custom-call(s32[4,2]{1,0:T(4,128)} %pad_add_fusion.3.table_ref, bf16[5120,1024]{1,0:T(8,128)(2,1)} %bitcast.81, bf16[2560,1024]{1,0:T(8,128)(2,1)} %get-tuple-element.70.resid_grad_ref, ...), custom_call_target="tpu_custom_call" | custom-call | flops 3758096384 | bytes 12582912 | tf_op jit(solution)/shard_map/first_backward/pallas_call | solution.py:878
  597.1 3.2 collective-permute-start.16
  602.7 5.4 broadcast.180.clone.1
  610.8 3.4 collective-permute-done.18
  615.8 6.2 collective-permute-done.19
  623.2 3.1 constant_dynamic-update-slice_fusion.2
  626.2 109.5 %collective-permute-done.20 = f32[24,1024]{1,0:T(8,128)S(1)} collective-permute-done((f32[24,1024]{1,0:T(8,128)S(1)}, f32[24,1024]{1,0:T(8,128)S(1)}, u32[]{:S(2)}, u32[]{:S(2)}) %collective-permute-start.20) | collective-permute-done | bytes 98336 | tf_op jit(solution)/shard_map/ppermute | solution.py:909
  740.7 3.1 constant_dynamic-update-slice_fusion
  743.8 4.6 slice_dynamic-update-slice_fusion
  (178 shorter events, 55.9 us)
Async XLA Ops:
  0.7 38.5 %copy-start.28 = (s32[5]{0:T(128)S(1)}, s32[5]{0:T(128)}, u32[]{:S(2)}) copy-start(s32[5]{0:T(128)} %param.22) | copy-start | bytes 64
  2.2 35.3 %collective-permute-start = (bf16[3,1024,256]{2,1,0:T(8,128)(2,1)S(1)}, bf16[3,1024,256]{2,1,0:T(8,128)(2,1)S(1)}, u32[]{:S(2)}, u32[]{:S(2)}) collective-permute-start(bf16[3,1024,256]{2,1,0:T(8,128)(2,1)S(1)} %constant_dynamic-slice_fusion.6), channel_id=1, source_target_pairs={{0,1},{1,0},{2,3},{3,2},{4,5},{5,4},{6,7},{7,6},{8,9},{9,8},{10,11... | collective-permute-start | bytes 4718600 | tf_op jit(solution)/shard_map/ppermute | solution.py:909
  2.5 135.2 %copy-start.26 = (s32[8]{0:T(128)}, s32[8]{0:T(128)S(1)}, u32[]{:S(2)}) copy-start(s32[8]{0:T(128)S(1)} %iota_add_fusion.5.table_ref) | copy-start | bytes 100
  37.5 101.4 %copy-start.1 = (bf16[3,1024,256]{2,1,0:T(8,128)(2,1)}, bf16[3,1024,256]{2,1,0:T(8,128)(2,1)S(1)}, u32[]{:S(2)}) copy-start(bf16[3,1024,256]{2,1,0:T(8,128)(2,1)S(1)} %collective-permute-done.refs_5_.near_ref) | copy-start | bytes 4718596
  37.5 12.2 %collective-permute-start.4 = (bf16[256,1024]{1,0:T(8,128)(2,1)}, bf16[256,1024]{1,0:T(8,128)(2,1)S(1)}, u32[]{:S(2)}, u32[]{:S(2)}) collective-permute-start(bf16[256,1024]{1,0:T(8,128)(2,1)} %constant_dynamic-slice_fusion.5), channel_id=1, source_target_pairs={{0,1},{1,0},{2,3},{3,2},{4,5},{5,4},{6,7},{7,6},{8,9},{9,8},{10,11... | collective-permute-start | bytes 1572872 | tf_op jit(solution)/shard_map/ppermute | solution.py:909
  39.9 103.1 %copy-start = (s32[2]{0:T(128)}, s32[2]{0:T(128)S(1)}, u32[]{:S(2)}) copy-start(s32[2]{0:T(128)S(1)} %dynamic_slice.35.lens_ref) | copy-start | bytes 28
  49.7 85.1 %collective-permute-start.6 = (bf16[1024,1024]{1,0:T(8,128)(2,1)}, bf16[1024,1024]{1,0:T(8,128)(2,1)}, u32[]{:S(2)}, u32[]{:S(2)}) collective-permute-start(bf16[1024,1024]{1,0:T(8,128)(2,1)} %constant_dynamic-slice_fusion.4), channel_id=1, source_target_pairs={{0,1},{1,0},{2,3},{3,2},{4,5},{5,4},{6,7},{7,6},{8,9},{9,8},{10,11... | collective-permute-start | bytes 6291464 | tf_op jit(solution)/shard_map/ppermute | solution.py:909
  129.6 120.9 %collective-permute-start.2 = (bf16[512,512]{1,0:T(8,128)(2,1)}, bf16[512,512]{1,0:T(8,128)(2,1)}, u32[]{:S(2)}, u32[]{:S(2)}) collective-permute-start(bf16[512,512]{1,0:T(8,128)(2,1)} %maximum_select_fusion.1), channel_id=1, source_target_pairs={{0,1},{1,0},{2,3},{3,2},{4,5},{5,4},{6,7},{7,6},{8,9},{9,8},{10,11... | collective-permute-start | bytes 1572872 | tf_op jit(solution)/shard_map/ppermute | solution.py:909
  133.3 60.8 %collective-permute-start.3 = (f32[2048]{0:T(1024)S(1)}, f32[2048]{0:T(1024)S(1)}, u32[]{:S(2)}, u32[]{:S(2)}) collective-permute-start(f32[2048]{0:T(1024)S(1)} %copy-done.24), channel_id=1, source_target_pairs={{0,1},{1,0},{2,3},{3,2},{4,5},{5,4},{6,7},{7,6},{8,9},{9,8},{10,11... | collective-permute-start | bytes 24584 | tf_op jit(solution)/shard_map/ppermute | solution.py:909
  134.8 52.1 %collective-permute-start.8 = (bf16[1024,1024]{1,0:T(8,128)(2,1)}, bf16[1024,1024]{1,0:T(8,128)(2,1)}, u32[]{:S(2)}, u32[]{:S(2)}) collective-permute-start(bf16[1024,1024]{1,0:T(8,128)(2,1)} %constant_dynamic-slice_fusion.3), channel_id=1, source_target_pairs={{0,1},{1,0},{2,3},{3,2},{4,5},{5,4},{6,7},{7,6},{8,9},{9,8},{10,11... | collective-permute-start | bytes 6291464 | tf_op jit(solution)/shard_map/ppermute | solution.py:909
  139.0 55.8 %collective-permute-start.1 = (bf16[3,1024,256]{2,1,0:T(8,128)(2,1)S(1)}, bf16[3,1024,256]{2,1,0:T(8,128)(2,1)S(1)}, u32[]{:S(2)}, u32[]{:S(2)}) collective-permute-start(bf16[3,1024,256]{2,1,0:T(8,128)(2,1)S(1)} %collective-permute-done.refs_5_.near_ref), channel_id=1, source_target_pairs={{0,2},{2,0},{4,6},{6,4},{8,10},{10,8},{12,14},{14,12},{16,18},{18,... | collective-permute-start | bytes 4718600 | tf_op jit(solution)/shard_map/ppermute | solution.py:917
  143.6 51.2 %copy-start.12 = (bf16[2,8,512]{2,1,0:T(8,128)(2,1)}, bf16[2,8,512]{2,1,0:T(8,128)(2,1)S(1)}, u32[]{:S(2)}) copy-start(bf16[2,8,512]{2,1,0:T(8,128)(2,1)S(1)} %maximum_select_fusion.3.refs_4_) | copy-start | bytes 49156
  144.2 109.7 %collective-permute-start.7 = (bf16[1024,1024]{1,0:T(8,128)(2,1)}, bf16[1024,1024]{1,0:T(8,128)(2,1)}, u32[]{:S(2)}, u32[]{:S(2)}) collective-permute-start(bf16[1024,1024]{1,0:T(8,128)(2,1)} %collective-permute-done.6.up_near), channel_id=1, source_target_pairs={{0,2},{2,0},{4,6},{6,4},{8,10},{10,8},{12,14},{14,12},{16,18},{18,... | collective-permute-start | bytes 6291464 | tf_op jit(solution)/shard_map/ppermute | solution.py:917
  186.9 67.1 %collective-permute-start.9 = (bf16[1024,1024]{1,0:T(8,128)(2,1)}, bf16[1024,1024]{1,0:T(8,128)(2,1)}, u32[]{:S(2)}, u32[]{:S(2)}) collective-permute-start(bf16[1024,1024]{1,0:T(8,128)(2,1)} %collective-permute-done.8.down_near), channel_id=1, source_target_pairs={{0,2},{2,0},{4,6},{6,4},{8,10},{10,8},{12,14},{14,12},{16,18},{18,... | collective-permute-start | bytes 6291464 | tf_op jit(solution)/shard_map/ppermute | solution.py:917
  194.8 59.2 %collective-permute-start.5 = (bf16[256,1024]{1,0:T(8,128)(2,1)}, bf16[256,1024]{1,0:T(8,128)(2,1)}, u32[]{:S(2)}, u32[]{:S(2)}) collective-permute-start(bf16[256,1024]{1,0:T(8,128)(2,1)} %copy-done.27), channel_id=1, source_target_pairs={{0,2},{2,0},{4,6},{6,4},{8,10},{10,8},{12,14},{14,12},{16,18},{18,... | collective-permute-start | bytes 1572872 | tf_op jit(solution)/shard_map/ppermute | solution.py:917
  367.5 134.3 %collective-permute-start.10 = (bf16[512,512]{1,0:T(8,128)(2,1)}, bf16[512,512]{1,0:T(8,128)(2,1)S(1)}, u32[]{:S(2)}, u32[]{:S(2)}) collective-permute-start(bf16[512,512]{1,0:T(8,128)(2,1)} %maximum_select_fusion.2), channel_id=1, source_target_pairs={{0,1},{1,0},{2,3},{3,2},{4,5},{5,4},{6,7},{7,6},{8,9},{9,8},{10,11... | collective-permute-start | bytes 1572872 | tf_op jit(solution)/shard_map/ppermute | solution.py:909
  441.3 181.8 %collective-permute-start.13 = (bf16[1024,1024]{1,0:T(8,128)(2,1)}, bf16[1024,1024]{1,0:T(8,128)(2,1)}, u32[]{:S(2)}, u32[]{:S(2)}) collective-permute-start(bf16[1024,1024]{1,0:T(8,128)(2,1)} %get-tuple-element.81), channel_id=1, source_target_pairs={{0,1},{1,0},{2,3},{3,2},{4,5},{5,4},{6,7},{7,6},{8,9},{9,8},{10,11... | collective-permute-start | bytes 6291464 | tf_op jit(solution)/shard_map/ppermute | solution.py:909
  520.4 59.6 %collective-permute-start.12 = (bf16[3,512,512]{2,1,0:T(8,128)(2,1)S(1)}, bf16[3,512,512]{2,1,0:T(8,128)(2,1)S(1)}, u32[]{:S(2)}, u32[]{:S(2)}) collective-permute-start(bf16[3,512,512]{2,1,0:T(8,128)(2,1)S(1)} %maximum_select_fusion), channel_id=1, source_target_pairs={{0,1},{1,0},{2,3},{3,2},{4,5},{5,4},{6,7},{7,6},{8,9},{9,8},{10,11... | collective-permute-start | bytes 4718600 | tf_op jit(solution)/shard_map/ppermute | solution.py:909
  549.8 194.0 %collective-permute-start.11 = (bf16[2560,1024]{1,0:T(8,128)(2,1)}, bf16[2560,1024]{1,0:T(8,128)(2,1)}, u32[]{:S(2)}, u32[]{:S(2)}) collective-permute-start(bf16[2560,1024]{1,0:T(8,128)(2,1)} %get-tuple-element.69), channel_id=1, source_target_pairs={{0,1},{1,0},{2,3},{3,2},{4,5},{5,4},{6,7},{7,6},{8,9},{9,8},{10,11... | collective-permute-start | bytes 15728648 | tf_op jit(solution)/shard_map/ppermute | solution.py:909
  572.0 168.7 %collective-permute-start.15 = (bf16[1024,1024]{1,0:T(8,128)(2,1)}, bf16[1024,1024]{1,0:T(8,128)(2,1)}, u32[]{:S(2)}, u32[]{:S(2)}) collective-permute-start(bf16[1024,1024]{1,0:T(8,128)(2,1)} %get-tuple-element.92), channel_id=1, source_target_pairs={{0,1},{1,0},{2,3},{3,2},{4,5},{5,4},{6,7},{7,6},{8,9},{9,8},{10,11... | collective-permute-start | bytes 6291464 | tf_op jit(solution)/shard_map/ppermute | solution.py:909
  597.1 5.5 collective-permute-start.16
  602.6 7.1 collective-permute-start.17
  609.7 128.8 %collective-permute-start.14 = (bf16[512,1024]{1,0:T(8,128)(2,1)S(1)}, bf16[512,1024]{1,0:T(8,128)(2,1)}, u32[]{:S(2)}, u32[]{:S(2)}) collective-permute-start(bf16[512,1024]{1,0:T(8,128)(2,1)S(1)} %copy-done.6), channel_id=1, source_target_pairs={{0,1},{1,0},{2,3},{3,2},{4,5},{5,4},{6,7},{7,6},{8,9},{9,8},{10,11... | collective-permute-start | bytes 3145736 | tf_op jit(solution)/shard_map/ppermute | solution.py:909
  609.7 4.5 collective-permute-start.18
  614.2 7.8 %collective-permute-start.19 = (f32[24,1024]{1,0:T(8,128)S(1)}, f32[24,1024]{1,0:T(8,128)S(1)}, u32[]{:S(2)}, u32[]{:S(2)}) collective-permute-start(f32[24,1024]{1,0:T(8,128)S(1)} %add.307), channel_id=1, source_target_pairs={{0,16},{2,18},{4,20},{6,22},{8,24},{10,26},{12,28},{14,30},{16,0},... | collective-permute-start | bytes 294920 | tf_op jit(solution)/shard_map/ppermute | solution.py:942
  615.8 121.3 %copy-start.9 = (f32[2,4,1024]{2,1,0:T(4,128)S(1)}, f32[2,4,1024]{2,1,0:T(4,128)}, u32[]{:S(2)}) copy-start(f32[2,4,1024]{2,1,0:T(4,128)} %param.35) | copy-start | bytes 98308
  615.8 121.3 %copy-start.14 = (f32[2,4,1024]{2,1,0:T(4,128)S(1)}, f32[2,4,1024]{2,1,0:T(4,128)}, u32[]{:S(2)}) copy-start(f32[2,4,1024]{2,1,0:T(4,128)} %param.37) | copy-start | bytes 98308
  615.8 121.3 %copy-start.15 = (f32[2,4,1024]{2,1,0:T(4,128)S(1)}, f32[2,4,1024]{2,1,0:T(4,128)}, u32[]{:S(2)}) copy-start(f32[2,4,1024]{2,1,0:T(4,128)} %param.39) | copy-start | bytes 98308
  615.8 122.0 %copy-start.11 = (f32[2,1024,4]{1,2,0:T(4,128)S(1)}, f32[2,1024,4]{1,2,0:T(4,128)}, u32[]{:S(2)}) copy-start(f32[2,1024,4]{1,2,0:T(4,128)} %param.34) | copy-start | bytes 98308
  615.8 122.0 %copy-start.16 = (f32[2,1024,4]{1,2,0:T(4,128)S(1)}, f32[2,1024,4]{1,2,0:T(4,128)}, u32[]{:S(2)}) copy-start(f32[2,1024,4]{1,2,0:T(4,128)} %param.36) | copy-start | bytes 98308
  615.8 122.0 %copy-start.17 = (f32[2,1024,4]{1,2,0:T(4,128)S(1)}, f32[2,1024,4]{1,2,0:T(4,128)}, u32[]{:S(2)}) copy-start(f32[2,1024,4]{1,2,0:T(4,128)} %param.38) | copy-start | bytes 98308
  622.0 113.8 %collective-permute-start.20 = (f32[24,1024]{1,0:T(8,128)S(1)}, f32[24,1024]{1,0:T(8,128)S(1)}, u32[]{:S(2)}, u32[]{:S(2)}) collective-permute-start(f32[24,1024]{1,0:T(8,128)S(1)} %add.308), channel_id=1, source_target_pairs={{0,1},{1,0},{2,3},{3,2},{4,5},{5,4},{6,7},{7,6},{8,9},{9,8},{10,11... | collective-permute-start | bytes 294920 | tf_op jit(solution)/shard_map/ppermute | solution.py:909
  (20 other events, 189.7 us)
